TPU v7x, 512 devices: a whole 4x4x16 slice. The times are simulated.
512 devices in a mesh: pop: 8 (over z_hi, x), blk: 64 (over z_lo, y, core).
Axes of the slice: x: 4, y: 4, z: 16 (z_hi: 2, z_lo: 8; z = z_hi * 8 + z_lo), core: 2. Of those that a mesh axis runs over, the one named last changes fastest.
Arguments:
- v_init: float32 [512, 2, 16384], P('pop', None, 'blk'), may hold values from -6 to 6
- a_init: float32 [512, 2, 16384], P('pop', None, 'blk'), may hold values from 0 to 1
- z_init: bfloat16 [512, 2, 16384], P('pop', None, 'blk'), may hold values from 0 to 1
- base_weight: bfloat16 [16384, 16384], P('blk', 'pop'), may hold values from -0.046875 to 0.046875
- factor_u: bfloat16 [512, 4, 16384], P('pop', None, 'blk'), may hold values from -6 to 6
- factor_v: bfloat16 [512, 4, 16384], P('pop', None, 'blk'), may hold values from -0.046875 to 0.046875
- in_weight: bfloat16 [700, 16384], P(None, 'blk'), may hold values from -0.21875 to 0.21875
- spikes_in: int32 [2, 2, 700], replicated, may hold values 0 or 1
- step_count: int32 [512, 2], P('pop'), may hold values from 1 to 2, as said below
- member_ids: int32 [512], P('pop'), may hold values from 0 to 511, each once
- decay_mem: float32 [16384], P('blk'), may hold values from 0.3 to 0.9
- decay_adapt: float32 [16384], P('blk'), may hold values from 0.5 to 0.95
- thr_base: float32 [16384], P('blk'), may hold values from 0.2 to 1
- thr_adapt: float32 [16384], P('blk'), may hold values from 0.5 to 2
Outputs:
- v_out: float32 [512, 2, 16384], P('pop', None, 'blk')
- a_out: float32 [512, 2, 16384], P('pop', None, 'blk')
Inputs may be any that keep to these rules, and one draw needn't show every extreme that they name: `member_ids`: each member appears in exactly one slot. `step_count`: a trial's state stops changing after its last step.
All inputs are finite; a program needn't handle non-finite values.
Results may differ from a plain program's by a relative error of at most 0.00088.
Values may be sent and summed in bfloat16 or wider, within the bound.
No kernel may reach another device: no remote copies, remote signals or barrier semaphores. Data moves between devices by JAX's collectives and lax.ppermute only.
A program may use at most 64 MiB of HBM per device.

v0:
```python
import functools

import jax
import jax.numpy as jnp
import numpy as np
from jax import lax
from jax.experimental import pallas as pl
from jax.experimental.pallas import tpu as pltpu
from jax.sharding import Mesh
from jax.sharding import PartitionSpec as P

STEPS = 2
AXES = ("zh", "x", "a", "b", "y", "c")
SIZES = (2, 4, 2, 4, 4, 2)
POP = ("zh", "x")
BLK = ("a", "b", "y", "c")
EXT = 8


def permute(value, dest):
    pairs = []
    for source in np.ndindex(*SIZES):
        there = dest(*source)
        pairs.append(
            (int(np.ravel_multi_index(source, SIZES)), int(np.ravel_multi_index(there, SIZES)))
        )
    return lax.ppermute(value, AXES, pairs)


def some(value, pick, dest):
    pairs = []
    for source in np.ndindex(*SIZES):
        if pick(*source):
            there = np.ravel_multi_index(dest(*source), SIZES)
            pairs.append((int(np.ravel_multi_index(source, SIZES)), int(there)))
    return lax.ppermute(value, AXES, pairs)


def to_owner(value):
    there = lambda zh, x, a, b, y, c: (a, x, zh, b, y, c)
    return some(value, lambda zh, x, a, b, y, c: zh != a, there)


def outward(value, middle):
    there = lambda zh, x, a, b, y, c: (zh, x, 1 - a, b, y, c)
    return some(value, lambda zh, x, a, b, y, c: (zh != a) == middle, there)


def over_b(value, k):
    return permute(value, lambda zh, x, a, b, y, c: (zh, x, a, b ^ k, y, c))


def over_y(value, k):
    return permute(value, lambda zh, x, a, b, y, c: (zh, x, a, b, y ^ k, c))


def over_c(value):
    return permute(value, lambda zh, x, a, b, y, c: (zh, x, a, b, y, 1 - c))


def over_x(value, k):
    return permute(value, lambda zh, x, a, b, y, c: (zh, x ^ k, a, b, y, c))


def over_zh(value):
    return permute(value, lambda zh, x, a, b, y, c: (1 - zh, x, a, b, y, c))


def member_mask(rows, cols, trials, rank):
    row = lax.broadcasted_iota(jnp.int32, (rows, cols), 0) // trials
    col = lax.broadcasted_iota(jnp.int32, (rows, cols), 1) // rank
    return row == col


def by_trial(values, rows):
    trials, block = values.shape
    trial = lax.broadcasted_iota(jnp.int32, (rows, block), 0) % trials
    out = jnp.broadcast_to(values[:1], (rows, block))
    for j in range(1, trials):
        out = jnp.where(trial == j, jnp.broadcast_to(values[j : j + 1], (rows, block)), out)
    return out


def three_terms(value):
    high = value.astype(jnp.bfloat16).astype(jnp.float32)
    rest = value - high
    middle = rest.astype(jnp.bfloat16).astype(jnp.float32)
    return [high, middle, rest - middle]


def store_packed(out_ref, spikes, factors, trials, rank):
    rows, block = spikes.shape
    full = lax.dot_general(
        spikes, factors, (((1,), (1,)), ((), ())), preferred_element_type=jnp.float32
    )
    kept = jnp.where(member_mask(rows, full.shape[1], trials, rank), full, 0.0)
    trial = lax.broadcasted_iota(jnp.int32, kept.shape, 0) % trials
    parts = [
        jnp.sum(jnp.where(trial == j, kept, 0.0), axis=0, keepdims=True) for j in range(trials)
    ]
    terms = three_terms(jnp.concatenate(parts, axis=0))
    pad = jnp.zeros((EXT - 3 * trials, block), jnp.float32)
    out_ref[:rows] = spikes
    out_ref[rows:] = jnp.concatenate([*terms, pad], axis=0).astype(jnp.bfloat16)


def pack_kernel(spikes_ref, factors_ref, out_ref, *, trials, rank):
    members, _, block = spikes_ref.shape
    spikes = spikes_ref[...].reshape(members * trials, block)
    store_packed(out_ref, spikes, factors_ref[...].reshape(members * rank, block), trials, rank)


def pack(spikes, factors):
    members, trials, block = spikes.shape
    rows, rank = members * trials, factors.shape[1]
    whole = pl.BlockSpec(memory_space=pltpu.VMEM)
    return pl.pallas_call(
        functools.partial(pack_kernel, trials=trials, rank=rank),
        out_shape=jax.ShapeDtypeStruct((rows + EXT, block), jnp.bfloat16),
        in_specs=[whole] * 2,
        out_specs=whole,
        compiler_params=pltpu.CompilerParams(vmem_limit_bytes=4 << 20),
        name="pack",
    )(spikes, factors)


def to_column(value, rows, trials):
    shape = (rows, value.shape[1])
    row = lax.broadcasted_iota(jnp.int32, shape, 0)
    kept = row // trials == lax.broadcasted_iota(jnp.int32, shape, 1)
    if value.shape[0] == 1:
        spread = jnp.broadcast_to(value, shape)
    else:
        spread = by_trial(value, rows)
    return jnp.sum(jnp.where(kept, spread, 0.0), axis=1, keepdims=True)


def update_kernel(*refs, step, trials, rank):
    mine_ref, theirs_ref, came_ref, packed_ref, v_ref, a_ref = refs[:6]
    lanes_ref, ids_ref, count_ref, u_ref, f_ref = refs[6:11]
    outs = refs[11:]
    members, _, block = u_ref.shape
    rows = members * trials
    total = mine_ref[:rows] + theirs_ref[:rows] + came_ref[:rows].astype(jnp.float32)
    tail = came_ref[rows:].astype(jnp.float32)
    proj = mine_ref[rows : rows + trials] + theirs_ref[rows : rows + trials]
    for term in range(3):
        proj = proj + tail[term * trials : (term + 1) * trials]
    mask = member_mask(rows, members * rank, trials, rank)
    spread = jnp.where(mask, by_trial(proj, rows), 0.0).astype(jnp.bfloat16)
    u_rows = u_ref[...].reshape(members * rank, block)
    low = jnp.dot(spread, u_rows, preferred_element_type=jnp.float32)
    current = by_trial(lanes_ref[4 + step * trials : 4 + (step + 1) * trials], rows)
    half_sign = to_column(0.5 - (ids_ref[...] & 1).astype(jnp.float32), rows, trials)
    count = to_column(count_ref[...].astype(jnp.float32), rows, trials)
    drive = total + half_sign * low + current
    decay_mem, decay_adapt = lanes_ref[0:1], lanes_ref[1:2]
    base, adapt = lanes_ref[2:3], lanes_ref[3:4]
    spikes = packed_ref[:rows].astype(jnp.float32)
    v, a = v_ref[...].reshape(rows, block), a_ref[...].reshape(rows, block)
    v_new = decay_mem * v + (1.0 - decay_mem) * drive - spikes * (base + adapt * a)
    v = jnp.where(count > float(step), v_new, v)
    outs[0][...] = v.reshape(outs[0].shape)
    if step + 1 < STEPS:
        a_new = decay_adapt * a + (1.0 - decay_adapt) * spikes
        a = jnp.where(count > float(step), a_new, a)
        fresh = jax.nn.sigmoid(3.0 * (v - base - adapt * a)).astype(jnp.bfloat16)
        f_rows = f_ref[...].reshape(members * rank, block)
        store_packed(outs[1], fresh, f_rows, trials, rank)
        outs[2][...] = a
        if step + 2 == STEPS:
            a_new = decay_adapt * a + (1.0 - decay_adapt) * fresh.astype(jnp.float32)
            a = jnp.where(count > float(step + 1), a_new, a)
            outs[3][...] = a.reshape(outs[3].shape)


def update(mine, theirs, came, packed, v, a, lanes, ids, count, factor_u, factor_v, step):
    members, rank, block = factor_u.shape
    trials = count.shape[0]
    rows = jax.ShapeDtypeStruct((members * trials, block), jnp.float32)
    final = jax.ShapeDtypeStruct((members, trials, block), jnp.float32)
    if step + 1 < STEPS:
        outs = [rows, jax.ShapeDtypeStruct(packed.shape, packed.dtype), rows]
        outs += [final] if step + 2 == STEPS else []
    else:
        outs = [final]
    whole = pl.BlockSpec(memory_space=pltpu.VMEM)
    return pl.pallas_call(
        functools.partial(update_kernel, step=step, trials=trials, rank=rank),
        out_shape=tuple(outs),
        in_specs=[whole] * 11,
        out_specs=(whole,) * len(outs),
        compiler_params=pltpu.CompilerParams(vmem_limit_bytes=6 << 20),
        name="update",
    )(mine, theirs, came, packed, v, a, lanes, ids, count, factor_u, factor_v)


def mix_kernel(at_ref, *refs, pieces, rows, trials):
    spikes, weights = refs[: 4 * pieces], refs[4 * pieces : 4 * pieces + 4]
    mine_ref, theirs_ref = refs[-2:]
    shift, y = at_ref[0], at_ref[1]
    block = spikes[0].shape[2]
    part = None
    for ref in spikes:
        for k in range(ref.shape[0]):
            tail = ref[k, rows:, :].astype(jnp.float32)
            part = tail if part is None else part + tail
    part = part[:trials] + part[trials : 2 * trials] + part[2 * trials : 3 * trials]

    def run(odd):
        total = None
        for q in range(4):
            for k in range(4):
                low, high = (k & 1) ^ odd, (shift >> 1) ^ (k >> 1)
                if pieces == 2:
                    chunk = spikes[q + 4 * low][high]
                else:
                    chunk = spikes[q][2 * low + high]
                piece = jnp.dot(
                    chunk, weights[k][y ^ q], preferred_element_type=jnp.float32
                )
                total = piece if total is None else total + piece
        for half, ref in enumerate((mine_ref, theirs_ref)):
            ref[...] = total[:, half * block : (half + 1) * block]
            ref[rows : rows + trials, :] = part

    for odd in range(2):
        pl.when((shift & 1) == odd)(functools.partial(run, odd))


def mix(at, spikes, weights, rows, trials):
    tall, block = spikes[0].shape[1:]
    out = jax.ShapeDtypeStruct((tall, block), jnp.float32)
    whole = pl.BlockSpec(memory_space=pltpu.VMEM)
    inputs = len(spikes) * spikes[0].size + 4 * weights[0].size
    return pl.pallas_call(
        functools.partial(mix_kernel, pieces=len(spikes) // 4, rows=rows, trials=trials),
        out_shape=(out, out),
        in_specs=[pl.BlockSpec(memory_space=pltpu.SMEM)] + [whole] * (len(spikes) + 4),
        out_specs=(whole, whole),
        cost_estimate=pl.CostEstimate(
            flops=8 * tall * weights[0].size,
            bytes_accessed=2 * inputs + 8 * tall * block,
            transcendentals=0,
        ),
        compiler_params=pltpu.CompilerParams(vmem_limit_bytes=12 << 20),
    )(at, *spikes, *weights)


def fold_kernel(mine_ref, theirs_ref, give_ref, *, rows, trials):
    give = mine_ref[...] + theirs_ref[...]
    terms = three_terms(give[rows : rows + trials])
    pad = jnp.zeros((EXT - 3 * trials, give.shape[1]), jnp.float32)
    give_ref[...] = jnp.concatenate([give[:rows], *terms, pad], axis=0).astype(jnp.bfloat16)


def fold(mine, theirs, rows, trials):
    whole = pl.BlockSpec(memory_space=pltpu.VMEM)
    return pl.pallas_call(
        functools.partial(fold_kernel, rows=rows, trials=trials),
        out_shape=jax.ShapeDtypeStruct(mine.shape, jnp.bfloat16),
        in_specs=[whole, whole],
        out_specs=whole,
        compiler_params=pltpu.CompilerParams(vmem_limit_bytes=4 << 20),
        name="fold",
    )(mine, theirs)


def spread_weights(base_weight, at):
    outs, depth = base_weight.shape
    block = depth // 8
    split = base_weight.reshape(outs, 4, 2, block)
    one = at["c"] == 1
    keep = jnp.where(one, split[:, :, 1], split[:, :, 0]).transpose(1, 2, 0)
    give = jnp.where(one, split[:, :, 0], split[:, :, 1]).transpose(1, 2, 0)
    got = over_c(give)
    own = jnp.concatenate([keep, got], axis=2)
    chunks = [own]
    for k in (1, 2, 3):
        chunks.append(over_x(own, k))
    return chunks


def body(
    v_init,
    a_init,
    z_init,
    base_weight,
    factor_u,
    factor_v,
    in_weight,
    spikes_in,
    step_count,
    member_ids,
    decay_mem,
    decay_adapt,
    thr_base,
    thr_adapt,
):
    members, trials, _ = v_init.shape
    rows = members * trials
    at = {name: lax.axis_index(name) for name in AXES}
    ids = member_ids.reshape(1, members)
    count = step_count.T
    current = jnp.dot(
        spikes_in.reshape(STEPS * trials, -1).astype(jnp.bfloat16),
        in_weight,
        preferred_element_type=jnp.float32,
    )
    lanes = jnp.stack([decay_mem, decay_adapt, thr_base, thr_adapt])
    lanes = jnp.concatenate([lanes, current], axis=0)
    place = jnp.stack([at["b"] ^ at["x"], at["y"]])
    outer = at["zh"] == at["a"]
    v, a = v_init, a_init
    packed = pack(z_init, factor_v)
    weights = spread_weights(base_weight, at)
    for step in range(STEPS):
        crossed = to_owner(packed)
        stayed = outward(packed, False)
        relayed = outward(crossed, True)
        keep = jnp.where(outer, packed, stayed)[None]
        give = jnp.where(outer, relayed, crossed)[None]
        keep = jnp.concatenate([keep, over_b(keep, 2)], axis=0)
        keep = [jnp.concatenate([keep, over_b(keep, 1)], axis=0)]
        half = [jnp.concatenate([give, over_b(give, 2)], axis=0)]
        if step == 0:
            half[0], place, lanes = lax.optimization_barrier((half[0], place, lanes))
        last = [over_b(half[0], 1)]
        for pieces, near, far in ((keep, 1, 3), (half, 3, 1)):
            came = {}
            for k in (near, far):
                came[k] = over_y(pieces[0], k)
            came[2] = over_y(came[near], far)
            pieces += [came[k] for k in (1, 2, 3)]
        for k in (1, 2, 3):
            last.append(over_y(last[0], k))
        mine, theirs = mix(place, half + last, weights, rows, trials)
        theirs = over_c(theirs)
        give = fold(mine, theirs, rows, trials)
        came = over_zh(give)
        mine, theirs = mix(place, keep, weights, rows, trials)
        theirs = over_c(theirs)
        v, *rest = update(
            mine, theirs, came, packed, v, a, lanes, ids, count, factor_u, factor_v, step
        )
        if rest:
            packed, a, *ends = rest
            a_out = ends[0] if ends else None
    return (v, a_out)


def solution(mesh):
    fine = Mesh(mesh.devices.reshape(SIZES), AXES)
    in_specs = (
        P(POP, None, BLK),
        P(POP, None, BLK),
        P(POP, None, BLK),
        P(BLK, POP),
        P(POP, None, BLK),
        P(POP, None, BLK),
        P(None, BLK),
        P(),
        P(POP, None),
        P(POP),
        P(BLK),
        P(BLK),
        P(BLK),
        P(BLK),
    )
    out_specs = (P(POP, None, BLK), P(POP, None, BLK))
    return jax.shard_map(body, mesh=fine, in_specs=in_specs, out_specs=out_specs, check_vma=False)
```

profile of v0, /device:TPU:1, one launch (start us, length us, event | category | flops | bytes accessed | tf_op | source)
XLA Modules:
  0.0 221.0 jit_solution(15007028626332750535)
XLA Ops:
  3.4 17.8 %collective-permute-start.3 = (bf16[136,256]{1,0:T(8,128)(2,1)S(1)}, bf16[136,256]{1,0:T(8,128)(2,1)S(1)}, u32[]{:S(2)}, u32[]{:S(2)}) collective-permute-start(bf16[136,256]{1,0:T(8,128)(2,1)S(1)} %pack.1.refs_3_), channel_id=1, source_target_pairs={{0,32},{1,33},{2,34},{3,35},{4,36},{5,37},{6,38},{7,39},{8,40},{9,... | collective-permute-start | bytes 208904 | tf_op jit(solution)/shard_map/ppermute | solution.py:36
  22.7 3.1 %collective-permute-start.9 = (bf16[4,256,256]{2,1,0:T(8,128)(2,1)S(1)}, bf16[4,256,256]{2,1,0:T(8,128)(2,1)S(1)}, u32[]{:S(2)}, u32[]{:S(2)}) collective-permute-start(bf16[4,256,256]{2,1,0:T(8,128)(2,1)S(1)} %get-tuple-element.33), channel_id=1, source_target_pairs={{0,1},{1,0},{2,3},{3,2},{4,5},{5,4},{6,7},{7,6},{8,9},{9,8},{10,11... | collective-permute-start | bytes 1572872 | tf_op jit(solution)/shard_map/ppermute | solution.py:27
  27.5 3.1 %collective-permute-start.4 = (bf16[1,136,256]{2,1,0:T(8,128)(2,1)S(1)}, bf16[1,136,256]{2,1,0:T(8,128)(2,1)S(1)}, u32[]{:S(2)}, u32[]{:S(2)}) collective-permute-start(bf16[1,136,256]{2,1,0:T(8,128)(2,1)S(1)} %select_bitcast_fusion.4), channel_id=1, source_target_pairs={{0,16},{1,17},{2,18},{3,19},{4,20},{5,21},{6,22},{7,23},{8,24},{9,... | collective-permute-start | bytes 208904 | tf_op jit(solution)/shard_map/ppermute | solution.py:27
  30.6 8.6 %collective-permute-done.1 = bf16[136,256]{1,0:T(8,128)(2,1)S(1)} collective-permute-done((bf16[136,256]{1,0:T(8,128)(2,1)S(1)}, bf16[136,256]{1,0:T(8,128)(2,1)S(1)}, u32[]{:S(2)}, u32[]{:S(2)}) %collective-permute-start.1) | collective-permute-done | bytes 69664 | tf_op jit(solution)/shard_map/ppermute | solution.py:36
  39.8 1.9 collective-permute-start.2
  42.5 2.7 %collective-permute-start.5 = (bf16[2,136,256]{2,1,0:T(8,128)(2,1)}, bf16[2,136,256]{2,1,0:T(8,128)(2,1)}, u32[]{:S(2)}, u32[]{:S(2)}) collective-permute-start(bf16[2,136,256]{2,1,0:T(8,128)(2,1)} %pad_maximum_fusion.4), channel_id=1, source_target_pairs={{0,8},{1,9},{2,10},{3,11},{4,12},{5,13},{6,14},{7,15},{8,0},{9,1},... | collective-permute-start | bytes 417800 | tf_op jit(solution)/shard_map/ppermute | solution.py:27
  45.3 3.1 %collective-permute-start.10 = (bf16[4,256,512]{2,1,0:T(8,128)(2,1)S(1)}, bf16[4,256,512]{2,1,0:T(8,128)(2,1)S(1)}, u32[]{:S(2)}, u32[]{:S(2)}) collective-permute-start(bf16[4,256,512]{2,1,0:T(8,128)(2,1)S(1)} %pad_maximum_fusion.refs_4_.refs_8_), channel_id=1, source_target_pairs={{0,64},{1,65},{2,66},{3,67},{4,68},{5,69},{6,70},{7,71},{8,72},{9,... | collective-permute-start | bytes 3145736 | tf_op jit(solution)/shard_map/ppermute | solution.py:27
  48.4 4.4 %collective-permute-start.11 = (bf16[4,256,512]{2,1,0:T(8,128)(2,1)S(1)}, bf16[4,256,512]{2,1,0:T(8,128)(2,1)S(1)}, u32[]{:S(2)}, u32[]{:S(2)}) collective-permute-start(bf16[4,256,512]{2,1,0:T(8,128)(2,1)S(1)} %pad_maximum_fusion.refs_4_.refs_8_), channel_id=1, source_target_pairs={{0,128},{1,129},{2,130},{3,131},{4,132},{5,133},{6,134},{7,135},{8... | collective-permute-start | bytes 3145736 | tf_op jit(solution)/shard_map/ppermute | solution.py:27
  52.8 2.1 collective-permute-start.12
  56.0 2.6 %collective-permute-start.17 = (bf16[2,136,256]{2,1,0:T(8,128)(2,1)S(1)}, bf16[2,136,256]{2,1,0:T(8,128)(2,1)S(1)}, u32[]{:S(2)}, u32[]{:S(2)}) collective-permute-start(bf16[2,136,256]{2,1,0:T(8,128)(2,1)S(1)} %pad_maximum_fusion.3.refs_0_), channel_id=1, source_target_pairs={{0,8},{1,9},{2,10},{3,11},{4,12},{5,13},{6,14},{7,15},{8,0},{9,1},... | collective-permute-start | bytes 417800 | tf_op jit(solution)/shard_map/ppermute | solution.py:27
  58.6 4.7 %collective-permute-start.15 = (bf16[2,136,256]{2,1,0:T(8,128)(2,1)S(1)}, bf16[2,136,256]{2,1,0:T(8,128)(2,1)S(1)}, u32[]{:S(2)}, u32[]{:S(2)}) collective-permute-start(bf16[2,136,256]{2,1,0:T(8,128)(2,1)S(1)} %pad_maximum_fusion.3.refs_0_), channel_id=1, source_target_pairs={{0,6},{1,7},{2,4},{3,5},{4,2},{5,3},{6,0},{7,1},{8,14},{9,15},{10,... | collective-permute-start | bytes 417800 | tf_op jit(solution)/shard_map/ppermute | solution.py:27
  63.3 2.1 collective-permute-start.14
  66.1 2.5 %collective-permute-start.18 = (bf16[2,136,256]{2,1,0:T(8,128)(2,1)S(1)}, bf16[2,136,256]{2,1,0:T(8,128)(2,1)S(1)}, u32[]{:S(2)}, u32[]{:S(2)}) collective-permute-start(bf16[2,136,256]{2,1,0:T(8,128)(2,1)S(1)} %collective-permute-done.17.refs_4_), channel_id=1, source_target_pairs={{0,2},{1,3},{2,0},{3,1},{4,6},{5,7},{6,4},{7,5},{8,10},{9,11},{10,... | collective-permute-start | bytes 417800 | tf_op jit(solution)/shard_map/ppermute | solution.py:27
  69.5 4.3 %collective-permute-start.19 = (bf16[2,136,256]{2,1,0:T(8,128)(2,1)S(1)}, bf16[2,136,256]{2,1,0:T(8,128)(2,1)S(1)}, u32[]{:S(2)}, u32[]{:S(2)}) collective-permute-start(bf16[2,136,256]{2,1,0:T(8,128)(2,1)S(1)} %collective-permute-done.17.refs_4_), channel_id=1, source_target_pairs={{0,4},{1,5},{2,6},{3,7},{4,0},{5,1},{6,2},{7,3},{8,12},{9,13},{10,... | collective-permute-start | bytes 417800 | tf_op jit(solution)/shard_map/ppermute | solution.py:27
  73.8 3.9 %collective-permute-start.20 = (bf16[2,136,256]{2,1,0:T(8,128)(2,1)S(1)}, bf16[2,136,256]{2,1,0:T(8,128)(2,1)S(1)}, u32[]{:S(2)}, u32[]{:S(2)}) collective-permute-start(bf16[2,136,256]{2,1,0:T(8,128)(2,1)S(1)} %collective-permute-done.17.refs_4_), channel_id=1, source_target_pairs={{0,6},{1,7},{2,4},{3,5},{4,2},{5,3},{6,0},{7,1},{8,14},{9,15},{10,... | collective-permute-start | bytes 417800 | tf_op jit(solution)/shard_map/ppermute | solution.py:27
  78.7 1.9 collective-permute-start.6
  80.6 2.1 collective-permute-done.20.refs_7_
  84.6 5.1 %collective-permute-done.16.refs_2_ = bf16[2,136,256]{2,1,0:T(8,128)(2,1)S(1)} collective-permute-done((bf16[2,136,256]{2,1,0:T(8,128)(2,1)S(1)}, bf16[2,136,256]{2,1,0:T(8,128)(2,1)S(1)}, u32[]{:S(2)}, u32[]{:S(2)}) %collective-permute-start.16) | collective-permute-done | bytes 139296 | tf_op jit(solution)/shard_map/ppermute | solution.py:27
  89.8 4.5 %collective-permute-start.8 = (bf16[4,136,256]{2,1,0:T(8,128)(2,1)S(1)}, bf16[4,136,256]{2,1,0:T(8,128)(2,1)S(1)}, u32[]{:S(2)}, u32[]{:S(2)}) collective-permute-start(bf16[4,136,256]{2,1,0:T(8,128)(2,1)S(1)} %pad_maximum_fusion.1.refs_0_), channel_id=1, source_target_pairs={{0,6},{1,7},{2,4},{3,5},{4,2},{5,3},{6,0},{7,1},{8,14},{9,15},{10,... | collective-permute-start | bytes 835592 | tf_op jit(solution)/shard_map/ppermute | solution.py:27
  94.3 2.0 collective-permute-start.7
  96.3 5.2 %collective-permute-done.12.refs_7_.refs_11_ = bf16[4,256,512]{2,1,0:T(8,128)(2,1)} collective-permute-done((bf16[4,256,512]{2,1,0:T(8,128)(2,1)S(1)}, bf16[4,256,512]{2,1,0:T(8,128)(2,1)}, u32[]{:S(2)}, u32[]{:S(2)}) %collective-permute-start.12) | collective-permute-done | bytes 1048608 | tf_op jit(solution)/shard_map/ppermute | solution.py:27
  101.5 2.0 shard_map.150
  103.6 4.6 %collective-permute-start.21 = (f32[136,256]{1,0:T(8,128)S(1)}, f32[136,256]{1,0:T(8,128)S(1)}, u32[]{:S(2)}, u32[]{:S(2)}) collective-permute-start(f32[136,256]{1,0:T(8,128)S(1)} %get-tuple-element.22), channel_id=1, source_target_pairs={{0,1},{1,0},{2,3},{3,2},{4,5},{5,4},{6,7},{7,6},{8,9},{9,8},{10,11... | collective-permute-start | bytes 417800 | tf_op jit(solution)/shard_map/ppermute | solution.py:27
  108.2 2.0 shard_map.149
  110.3 2.9 %collective-permute-start.13 = (f32[136,256]{1,0:T(8,128)S(1)}, f32[136,256]{1,0:T(8,128)S(1)}, u32[]{:S(2)}, u32[]{:S(2)}) collective-permute-start(f32[136,256]{1,0:T(8,128)S(1)} %get-tuple-element.19), channel_id=1, source_target_pairs={{0,1},{1,0},{2,3},{3,2},{4,5},{5,4},{6,7},{7,6},{8,9},{9,8},{10,11... | collective-permute-start | bytes 417800 | tf_op jit(solution)/shard_map/ppermute | solution.py:27
  113.2 3.4 %collective-permute-start.22 = (bf16[136,256]{1,0:T(8,128)(2,1)S(1)}, bf16[136,256]{1,0:T(8,128)(2,1)S(1)}, u32[]{:S(2)}, u32[]{:S(2)}) collective-permute-start(bf16[136,256]{1,0:T(8,128)(2,1)S(1)} %fold.2), channel_id=1, source_target_pairs={{0,256},{1,257},{2,258},{3,259},{4,260},{5,261},{6,262},{7,263},{8... | collective-permute-start | bytes 208904 | tf_op jit(solution)/shard_map/ppermute | solution.py:27
  116.7 12.5 %collective-permute-done.22.refs_2_ = bf16[136,256]{1,0:T(8,128)(2,1)S(1)} collective-permute-done((bf16[136,256]{1,0:T(8,128)(2,1)S(1)}, bf16[136,256]{1,0:T(8,128)(2,1)S(1)}, u32[]{:S(2)}, u32[]{:S(2)}) %collective-permute-start.22) | collective-permute-done | bytes 69664 | tf_op jit(solution)/shard_map/ppermute | solution.py:27
  132.8 6.1 %collective-permute-start.24 = (bf16[1,136,256]{2,1,0:T(8,128)(2,1)S(1)}, bf16[1,136,256]{2,1,0:T(8,128)(2,1)S(1)}, u32[]{:S(2)}, u32[]{:S(2)}) collective-permute-start(bf16[1,136,256]{2,1,0:T(8,128)(2,1)S(1)} %select_bitcast_fusion.3), channel_id=1, source_target_pairs={{0,16},{1,17},{2,18},{3,19},{4,20},{5,21},{6,22},{7,23},{8,24},{9,... | collective-permute-start | bytes 208904 | tf_op jit(solution)/shard_map/ppermute | solution.py:27
  141.3 2.0 collective-permute-start.25
  143.3 6.3 %collective-permute-done.31 = bf16[136,256]{1,0:T(8,128)(2,1)S(1)} collective-permute-done((bf16[136,256]{1,0:T(8,128)(2,1)S(1)}, bf16[136,256]{1,0:T(8,128)(2,1)S(1)}, u32[]{:S(2)}, u32[]{:S(2)}) %collective-permute-start.31) | collective-permute-done | bytes 69664 | tf_op jit(solution)/shard_map/ppermute | solution.py:36
  149.6 2.7 %collective-permute-start.32 = (bf16[1,136,256]{2,1,0:T(8,128)(2,1)S(1)}, bf16[1,136,256]{2,1,0:T(8,128)(2,1)S(1)}, u32[]{:S(2)}, u32[]{:S(2)}) collective-permute-start(bf16[1,136,256]{2,1,0:T(8,128)(2,1)S(1)} %select_bitcast_fusion.2), channel_id=1, source_target_pairs={{0,16},{1,17},{2,18},{3,19},{4,20},{5,21},{6,22},{7,23},{8,24},{9,... | collective-permute-start | bytes 208904 | tf_op jit(solution)/shard_map/ppermute | solution.py:27
  152.4 1.9 collective-permute-start.26
  155.6 2.9 %collective-permute-start.34 = (bf16[2,136,256]{2,1,0:T(8,128)(2,1)S(1)}, bf16[2,136,256]{2,1,0:T(8,128)(2,1)S(1)}, u32[]{:S(2)}, u32[]{:S(2)}) collective-permute-start(bf16[2,136,256]{2,1,0:T(8,128)(2,1)S(1)} %pad_maximum_fusion.6.refs_0_), channel_id=1, source_target_pairs={{0,6},{1,7},{2,4},{3,5},{4,2},{5,3},{6,0},{7,1},{8,14},{9,15},{10,... | collective-permute-start | bytes 417800 | tf_op jit(solution)/shard_map/ppermute | solution.py:27
  158.5 4.5 %collective-permute-start.36 = (bf16[2,136,256]{2,1,0:T(8,128)(2,1)S(1)}, bf16[2,136,256]{2,1,0:T(8,128)(2,1)S(1)}, u32[]{:S(2)}, u32[]{:S(2)}) collective-permute-start(bf16[2,136,256]{2,1,0:T(8,128)(2,1)S(1)} %pad_maximum_fusion.6.refs_0_), channel_id=1, source_target_pairs={{0,8},{1,9},{2,10},{3,11},{4,12},{5,13},{6,14},{7,15},{8,0},{9,1},... | collective-permute-start | bytes 417800 | tf_op jit(solution)/shard_map/ppermute | solution.py:27
  163.0 1.9 collective-permute-start.33
  164.9 3.4 %collective-permute-start.35 = (bf16[2,136,256]{2,1,0:T(8,128)(2,1)S(1)}, bf16[2,136,256]{2,1,0:T(8,128)(2,1)S(1)}, u32[]{:S(2)}, u32[]{:S(2)}) collective-permute-start(bf16[2,136,256]{2,1,0:T(8,128)(2,1)S(1)} %collective-permute-done.34.refs_3_), channel_id=1, source_target_pairs={{0,2},{1,3},{2,0},{3,1},{4,6},{5,7},{6,4},{7,5},{8,10},{9,11},{10,... | collective-permute-start | bytes 417800 | tf_op jit(solution)/shard_map/ppermute | solution.py:27
  168.3 1.9 collective-permute-start.28
  170.2 4.6 %collective-permute-start.27 = (bf16[4,136,256]{2,1,0:T(8,128)(2,1)S(1)}, bf16[4,136,256]{2,1,0:T(8,128)(2,1)S(1)}, u32[]{:S(2)}, u32[]{:S(2)}) collective-permute-start(bf16[4,136,256]{2,1,0:T(8,128)(2,1)S(1)} %collective-permute-done.26.refs_1_), channel_id=1, source_target_pairs={{0,6},{1,7},{2,4},{3,5},{4,2},{5,3},{6,0},{7,1},{8,14},{9,15},{10,... | collective-permute-start | bytes 835592 | tf_op jit(solution)/shard_map/ppermute | solution.py:27
  174.8 1.9 collective-permute-start.37
  176.8 3.1 %collective-permute-start.38 = (bf16[2,136,256]{2,1,0:T(8,128)(2,1)S(1)}, bf16[2,136,256]{2,1,0:T(8,128)(2,1)S(1)}, u32[]{:S(2)}, u32[]{:S(2)}) collective-permute-start(bf16[2,136,256]{2,1,0:T(8,128)(2,1)S(1)} %collective-permute-done.36.refs_4_), channel_id=1, source_target_pairs={{0,4},{1,5},{2,6},{3,7},{4,0},{5,1},{6,2},{7,3},{8,12},{9,13},{10,... | collective-permute-start | bytes 417800 | tf_op jit(solution)/shard_map/ppermute | solution.py:27
  179.9 4.6 %collective-permute-start.39 = (bf16[2,136,256]{2,1,0:T(8,128)(2,1)S(1)}, bf16[2,136,256]{2,1,0:T(8,128)(2,1)S(1)}, u32[]{:S(2)}, u32[]{:S(2)}) collective-permute-start(bf16[2,136,256]{2,1,0:T(8,128)(2,1)S(1)} %collective-permute-done.36.refs_4_), channel_id=1, source_target_pairs={{0,6},{1,7},{2,4},{3,5},{4,2},{5,3},{6,0},{7,1},{8,14},{9,15},{10,... | collective-permute-start | bytes 417800 | tf_op jit(solution)/shard_map/ppermute | solution.py:27
  184.5 4.2 %collective-permute-done.39.refs_7_ = bf16[2,136,256]{2,1,0:T(8,128)(2,1)S(1)} collective-permute-done((bf16[2,136,256]{2,1,0:T(8,128)(2,1)S(1)}, bf16[2,136,256]{2,1,0:T(8,128)(2,1)S(1)}, u32[]{:S(2)}, u32[]{:S(2)}) %collective-permute-start.39) | collective-permute-done | bytes 139296 | tf_op jit(solution)/shard_map/ppermute | solution.py:27
  188.7 2.0 shard_map.152
  190.7 8.4 %collective-permute-start.40 = (f32[136,256]{1,0:T(8,128)S(1)}, f32[136,256]{1,0:T(8,128)S(1)}, u32[]{:S(2)}, u32[]{:S(2)}) collective-permute-start(f32[136,256]{1,0:T(8,128)S(1)} %get-tuple-element.28), channel_id=1, source_target_pairs={{0,1},{1,0},{2,3},{3,2},{4,5},{5,4},{6,7},{7,6},{8,9},{9,8},{10,11... | collective-permute-start | bytes 417800 | tf_op jit(solution)/shard_map/ppermute | solution.py:27
  199.2 2.0 shard_map.151
  201.2 1.9 collective-permute-start.29
  203.2 4.3 %collective-permute-start.41 = (bf16[136,256]{1,0:T(8,128)(2,1)S(1)}, bf16[136,256]{1,0:T(8,128)(2,1)S(1)}, u32[]{:S(2)}, u32[]{:S(2)}) collective-permute-start(bf16[136,256]{1,0:T(8,128)(2,1)S(1)} %fold.3), channel_id=1, source_target_pairs={{0,256},{1,257},{2,258},{3,259},{4,260},{5,261},{6,262},{7,263},{8... | collective-permute-start | bytes 208904 | tf_op jit(solution)/shard_map/ppermute | solution.py:27
  207.4 12.7 %collective-permute-done.41.refs_2_ = bf16[136,256]{1,0:T(8,128)(2,1)S(1)} collective-permute-done((bf16[136,256]{1,0:T(8,128)(2,1)S(1)}, bf16[136,256]{1,0:T(8,128)(2,1)S(1)}, u32[]{:S(2)}, u32[]{:S(2)}) %collective-permute-start.41) | collective-permute-done | bytes 69664 | tf_op jit(solution)/shard_map/ppermute | solution.py:27
  (99 shorter events, 21.1 us)
Async XLA Ops:
  2.7 23.4 %collective-permute-start = (bf16[136,256]{1,0:T(8,128)(2,1)S(1)}, bf16[136,256]{1,0:T(8,128)(2,1)S(1)}, u32[]{:S(2)}, u32[]{:S(2)}) collective-permute-start(bf16[136,256]{1,0:T(8,128)(2,1)S(1)} %pack.1.refs_3_), channel_id=1, source_target_pairs={{32,256},{33,257},{34,258},{35,259},{36,260},{37,261},{38,262},{39... | collective-permute-start | bytes 208904 | tf_op jit(solution)/shard_map/ppermute | solution.py:36
  3.4 24.1 %collective-permute-start.3 = (bf16[136,256]{1,0:T(8,128)(2,1)S(1)}, bf16[136,256]{1,0:T(8,128)(2,1)S(1)}, u32[]{:S(2)}, u32[]{:S(2)}) collective-permute-start(bf16[136,256]{1,0:T(8,128)(2,1)S(1)} %pack.1.refs_3_), channel_id=1, source_target_pairs={{0,32},{1,33},{2,34},{3,35},{4,36},{5,37},{6,38},{7,39},{8,40},{9,... | collective-permute-start | bytes 208904 | tf_op jit(solution)/shard_map/ppermute | solution.py:36
  22.7 22.4 %collective-permute-start.9 = (bf16[4,256,256]{2,1,0:T(8,128)(2,1)S(1)}, bf16[4,256,256]{2,1,0:T(8,128)(2,1)S(1)}, u32[]{:S(2)}, u32[]{:S(2)}) collective-permute-start(bf16[4,256,256]{2,1,0:T(8,128)(2,1)S(1)} %get-tuple-element.33), channel_id=1, source_target_pairs={{0,1},{1,0},{2,3},{3,2},{4,5},{5,4},{6,7},{7,6},{8,9},{9,8},{10,11... | collective-permute-start | bytes 1572872 | tf_op jit(solution)/shard_map/ppermute | solution.py:27
  26.1 13.1 %collective-permute-start.1 = (bf16[136,256]{1,0:T(8,128)(2,1)S(1)}, bf16[136,256]{1,0:T(8,128)(2,1)S(1)}, u32[]{:S(2)}, u32[]{:S(2)}) collective-permute-start(bf16[136,256]{1,0:T(8,128)(2,1)S(1)} %collective-permute-done), channel_id=1, source_target_pairs={{32,0},{33,1},{34,2},{35,3},{36,4},{37,5},{38,6},{39,7},{40,8},{41... | collective-permute-start | bytes 208904 | tf_op jit(solution)/shard_map/ppermute | solution.py:36
  27.5 14.3 %collective-permute-start.4 = (bf16[1,136,256]{2,1,0:T(8,128)(2,1)S(1)}, bf16[1,136,256]{2,1,0:T(8,128)(2,1)S(1)}, u32[]{:S(2)}, u32[]{:S(2)}) collective-permute-start(bf16[1,136,256]{2,1,0:T(8,128)(2,1)S(1)} %select_bitcast_fusion.4), channel_id=1, source_target_pairs={{0,16},{1,17},{2,18},{3,19},{4,20},{5,21},{6,22},{7,23},{8,24},{9,... | collective-permute-start | bytes 208904 | tf_op jit(solution)/shard_map/ppermute | solution.py:27
  39.8 15.2 %collective-permute-start.2 = (bf16[1,136,256]{2,1,0:T(8,128)(2,1)}, bf16[1,136,256]{2,1,0:T(8,128)(2,1)}, u32[]{:S(2)}, u32[]{:S(2)}) collective-permute-start(bf16[1,136,256]{2,1,0:T(8,128)(2,1)} %select_bitcast_fusion.5), channel_id=1, source_target_pairs={{0,16},{1,17},{2,18},{3,19},{4,20},{5,21},{6,22},{7,23},{8,24},{9,... | collective-permute-start | bytes 208904 | tf_op jit(solution)/shard_map/ppermute | solution.py:27
  42.5 16.1 %collective-permute-start.5 = (bf16[2,136,256]{2,1,0:T(8,128)(2,1)}, bf16[2,136,256]{2,1,0:T(8,128)(2,1)}, u32[]{:S(2)}, u32[]{:S(2)}) collective-permute-start(bf16[2,136,256]{2,1,0:T(8,128)(2,1)} %pad_maximum_fusion.4), channel_id=1, source_target_pairs={{0,8},{1,9},{2,10},{3,11},{4,12},{5,13},{6,14},{7,15},{8,0},{9,1},... | collective-permute-start | bytes 417800 | tf_op jit(solution)/shard_map/ppermute | solution.py:27
  45.3 51.0 %collective-permute-start.10 = (bf16[4,256,512]{2,1,0:T(8,128)(2,1)S(1)}, bf16[4,256,512]{2,1,0:T(8,128)(2,1)S(1)}, u32[]{:S(2)}, u32[]{:S(2)}) collective-permute-start(bf16[4,256,512]{2,1,0:T(8,128)(2,1)S(1)} %pad_maximum_fusion.refs_4_.refs_8_), channel_id=1, source_target_pairs={{0,64},{1,65},{2,66},{3,67},{4,68},{5,69},{6,70},{7,71},{8,72},{9,... | collective-permute-start | bytes 3145736 | tf_op jit(solution)/shard_map/ppermute | solution.py:27
  48.4 47.8 %collective-permute-start.11 = (bf16[4,256,512]{2,1,0:T(8,128)(2,1)S(1)}, bf16[4,256,512]{2,1,0:T(8,128)(2,1)S(1)}, u32[]{:S(2)}, u32[]{:S(2)}) collective-permute-start(bf16[4,256,512]{2,1,0:T(8,128)(2,1)S(1)} %pad_maximum_fusion.refs_4_.refs_8_), channel_id=1, source_target_pairs={{0,128},{1,129},{2,130},{3,131},{4,132},{5,133},{6,134},{7,135},{8... | collective-permute-start | bytes 3145736 | tf_op jit(solution)/shard_map/ppermute | solution.py:27
  52.8 48.7 %collective-permute-start.12 = (bf16[4,256,512]{2,1,0:T(8,128)(2,1)S(1)}, bf16[4,256,512]{2,1,0:T(8,128)(2,1)}, u32[]{:S(2)}, u32[]{:S(2)}) collective-permute-start(bf16[4,256,512]{2,1,0:T(8,128)(2,1)S(1)} %pad_maximum_fusion.refs_4_.refs_8_), channel_id=1, source_target_pairs={{0,192},{1,193},{2,194},{3,195},{4,196},{5,197},{6,198},{7,199},{8... | collective-permute-start | bytes 3145736 | tf_op jit(solution)/shard_map/ppermute | solution.py:27
  56.0 7.3 %collective-permute-start.17 = (bf16[2,136,256]{2,1,0:T(8,128)(2,1)S(1)}, bf16[2,136,256]{2,1,0:T(8,128)(2,1)S(1)}, u32[]{:S(2)}, u32[]{:S(2)}) collective-permute-start(bf16[2,136,256]{2,1,0:T(8,128)(2,1)S(1)} %pad_maximum_fusion.3.refs_0_), channel_id=1, source_target_pairs={{0,8},{1,9},{2,10},{3,11},{4,12},{5,13},{6,14},{7,15},{8,0},{9,1},... | collective-permute-start | bytes 417800 | tf_op jit(solution)/shard_map/ppermute | solution.py:27
  58.6 7.5 %collective-permute-start.15 = (bf16[2,136,256]{2,1,0:T(8,128)(2,1)S(1)}, bf16[2,136,256]{2,1,0:T(8,128)(2,1)S(1)}, u32[]{:S(2)}, u32[]{:S(2)}) collective-permute-start(bf16[2,136,256]{2,1,0:T(8,128)(2,1)S(1)} %pad_maximum_fusion.3.refs_0_), channel_id=1, source_target_pairs={{0,6},{1,7},{2,4},{3,5},{4,2},{5,3},{6,0},{7,1},{8,14},{9,15},{10,... | collective-permute-start | bytes 417800 | tf_op jit(solution)/shard_map/ppermute | solution.py:27
  63.3 6.2 %collective-permute-start.14 = (bf16[2,136,256]{2,1,0:T(8,128)(2,1)S(1)}, bf16[2,136,256]{2,1,0:T(8,128)(2,1)S(1)}, u32[]{:S(2)}, u32[]{:S(2)}) collective-permute-start(bf16[2,136,256]{2,1,0:T(8,128)(2,1)S(1)} %pad_maximum_fusion.3.refs_0_), channel_id=1, source_target_pairs={{0,2},{1,3},{2,0},{3,1},{4,6},{5,7},{6,4},{7,5},{8,10},{9,11},{10,... | collective-permute-start | bytes 417800 | tf_op jit(solution)/shard_map/ppermute | solution.py:27
  66.1 7.7 %collective-permute-start.18 = (bf16[2,136,256]{2,1,0:T(8,128)(2,1)S(1)}, bf16[2,136,256]{2,1,0:T(8,128)(2,1)S(1)}, u32[]{:S(2)}, u32[]{:S(2)}) collective-permute-start(bf16[2,136,256]{2,1,0:T(8,128)(2,1)S(1)} %collective-permute-done.17.refs_4_), channel_id=1, source_target_pairs={{0,2},{1,3},{2,0},{3,1},{4,6},{5,7},{6,4},{7,5},{8,10},{9,11},{10,... | collective-permute-start | bytes 417800 | tf_op jit(solution)/shard_map/ppermute | solution.py:27
  69.5 9.2 %collective-permute-start.19 = (bf16[2,136,256]{2,1,0:T(8,128)(2,1)S(1)}, bf16[2,136,256]{2,1,0:T(8,128)(2,1)S(1)}, u32[]{:S(2)}, u32[]{:S(2)}) collective-permute-start(bf16[2,136,256]{2,1,0:T(8,128)(2,1)S(1)} %collective-permute-done.17.refs_4_), channel_id=1, source_target_pairs={{0,4},{1,5},{2,6},{3,7},{4,0},{5,1},{6,2},{7,3},{8,12},{9,13},{10,... | collective-permute-start | bytes 417800 | tf_op jit(solution)/shard_map/ppermute | solution.py:27
  73.8 8.9 %collective-permute-start.20 = (bf16[2,136,256]{2,1,0:T(8,128)(2,1)S(1)}, bf16[2,136,256]{2,1,0:T(8,128)(2,1)S(1)}, u32[]{:S(2)}, u32[]{:S(2)}) collective-permute-start(bf16[2,136,256]{2,1,0:T(8,128)(2,1)S(1)} %collective-permute-done.17.refs_4_), channel_id=1, source_target_pairs={{0,6},{1,7},{2,4},{3,5},{4,2},{5,3},{6,0},{7,1},{8,14},{9,15},{10,... | collective-permute-start | bytes 417800 | tf_op jit(solution)/shard_map/ppermute | solution.py:27
  78.7 15.5 %collective-permute-start.6 = (bf16[4,136,256]{2,1,0:T(8,128)(2,1)S(1)}, bf16[4,136,256]{2,1,0:T(8,128)(2,1)S(1)}, u32[]{:S(2)}, u32[]{:S(2)}) collective-permute-start(bf16[4,136,256]{2,1,0:T(8,128)(2,1)S(1)} %pad_maximum_fusion.1.refs_0_), channel_id=1, source_target_pairs={{0,2},{1,3},{2,0},{3,1},{4,6},{5,7},{6,4},{7,5},{8,10},{9,11},{10,... | collective-permute-start | bytes 835592 | tf_op jit(solution)/shard_map/ppermute | solution.py:27
  82.7 7.1 %collective-permute-start.16 = (bf16[2,136,256]{2,1,0:T(8,128)(2,1)S(1)}, bf16[2,136,256]{2,1,0:T(8,128)(2,1)S(1)}, u32[]{:S(2)}, u32[]{:S(2)}) collective-permute-start(bf16[2,136,256]{2,1,0:T(8,128)(2,1)S(1)} %collective-permute-done.15.refs_3_), channel_id=1, source_target_pairs={{0,2},{1,3},{2,0},{3,1},{4,6},{5,7},{6,4},{7,5},{8,10},{9,11},{10,... | collective-permute-start | bytes 417800 | tf_op jit(solution)/shard_map/ppermute | solution.py:27
  89.8 18.5 %collective-permute-start.8 = (bf16[4,136,256]{2,1,0:T(8,128)(2,1)S(1)}, bf16[4,136,256]{2,1,0:T(8,128)(2,1)S(1)}, u32[]{:S(2)}, u32[]{:S(2)}) collective-permute-start(bf16[4,136,256]{2,1,0:T(8,128)(2,1)S(1)} %pad_maximum_fusion.1.refs_0_), channel_id=1, source_target_pairs={{0,6},{1,7},{2,4},{3,5},{4,2},{5,3},{6,0},{7,1},{8,14},{9,15},{10,... | collective-permute-start | bytes 835592 | tf_op jit(solution)/shard_map/ppermute | solution.py:27
  94.3 14.0 %collective-permute-start.7 = (bf16[4,136,256]{2,1,0:T(8,128)(2,1)S(1)}, bf16[4,136,256]{2,1,0:T(8,128)(2,1)S(1)}, u32[]{:S(2)}, u32[]{:S(2)}) collective-permute-start(bf16[4,136,256]{2,1,0:T(8,128)(2,1)S(1)} %collective-permute-done.6.refs_1_), channel_id=1, source_target_pairs={{0,6},{1,7},{2,4},{3,5},{4,2},{5,3},{6,0},{7,1},{8,14},{9,15},{10,... | collective-permute-start | bytes 835592 | tf_op jit(solution)/shard_map/ppermute | solution.py:27
  103.5 25.6 %copy-start.2 = (bf16[64,4,256]{2,1,0:T(4,128)(2,1)S(1)}, bf16[64,4,256]{2,1,0:T(4,128)(2,1)}, u32[]{:S(2)}) copy-start(bf16[64,4,256]{2,1,0:T(4,128)(2,1)} %refs_10_.3) | copy-start | bytes 393220
  103.5 25.6 %copy-start.4 = (bf16[136,256]{1,0:T(8,128)(2,1)S(1)}, bf16[136,256]{1,0:T(8,128)(2,1)}, u32[]{:S(2)}) copy-start(bf16[136,256]{1,0:T(8,128)(2,1)} %copy-done.3) | copy-start | bytes 208900
  103.5 25.6 %copy-start.5 = (bf16[64,4,256]{2,1,0:T(4,128)(2,1)S(1)}, bf16[64,4,256]{2,1,0:T(4,128)(2,1)}, u32[]{:S(2)}) copy-start(bf16[64,4,256]{2,1,0:T(4,128)(2,1)} %refs_9_.3) | copy-start | bytes 393220
  103.6 25.6 %copy-start.6 = (f32[64,2,256]{2,1,0:T(2,128)S(1)}, f32[64,2,256]{2,1,0:T(2,128)}, u32[]{:S(2)}) copy-start(f32[64,2,256]{2,1,0:T(2,128)} %refs_4_.1) | copy-start | bytes 393220
  103.6 25.6 %copy-start.7 = (f32[64,2,256]{2,1,0:T(2,128)S(1)}, f32[64,2,256]{2,1,0:T(2,128)}, u32[]{:S(2)}) copy-start(f32[64,2,256]{2,1,0:T(2,128)} %refs_5_.1) | copy-start | bytes 393220
  103.6 25.6 %copy-start.9 = (s32[64,2]{0,1:T(2,128)S(1)}, s32[64,2]{0,1:T(2,128)}, u32[]{:S(2)}) copy-start(s32[64,2]{0,1:T(2,128)} %param.22) | copy-start | bytes 1540
  103.6 9.6 %collective-permute-start.21 = (f32[136,256]{1,0:T(8,128)S(1)}, f32[136,256]{1,0:T(8,128)S(1)}, u32[]{:S(2)}, u32[]{:S(2)}) collective-permute-start(f32[136,256]{1,0:T(8,128)S(1)} %get-tuple-element.22), channel_id=1, source_target_pairs={{0,1},{1,0},{2,3},{3,2},{4,5},{5,4},{6,7},{7,6},{8,9},{9,8},{10,11... | collective-permute-start | bytes 417800 | tf_op jit(solution)/shard_map/ppermute | solution.py:27
  110.3 6.4 %collective-permute-start.13 = (f32[136,256]{1,0:T(8,128)S(1)}, f32[136,256]{1,0:T(8,128)S(1)}, u32[]{:S(2)}, u32[]{:S(2)}) collective-permute-start(f32[136,256]{1,0:T(8,128)S(1)} %get-tuple-element.19), channel_id=1, source_target_pairs={{0,1},{1,0},{2,3},{3,2},{4,5},{5,4},{6,7},{7,6},{8,9},{9,8},{10,11... | collective-permute-start | bytes 417800 | tf_op jit(solution)/shard_map/ppermute | solution.py:27
  113.2 15.9 %collective-permute-start.22 = (bf16[136,256]{1,0:T(8,128)(2,1)S(1)}, bf16[136,256]{1,0:T(8,128)(2,1)S(1)}, u32[]{:S(2)}, u32[]{:S(2)}) collective-permute-start(bf16[136,256]{1,0:T(8,128)(2,1)S(1)} %fold.2), channel_id=1, source_target_pairs={{0,256},{1,257},{2,258},{3,259},{4,260},{5,261},{6,262},{7,263},{8... | collective-permute-start | bytes 208904 | tf_op jit(solution)/shard_map/ppermute | solution.py:27
  130.1 2.6 %collective-permute-start.23 = (bf16[136,256]{1,0:T(8,128)(2,1)S(1)}, bf16[136,256]{1,0:T(8,128)(2,1)S(1)}, u32[]{:S(2)}, u32[]{:S(2)}) collective-permute-start(bf16[136,256]{1,0:T(8,128)(2,1)S(1)} %get-tuple-element.24.refs_3_), channel_id=1, source_target_pairs={{0,32},{1,33},{2,34},{3,35},{4,36},{5,37},{6,38},{7,39},{8,40},{9,... | collective-permute-start | bytes 208904 | tf_op jit(solution)/shard_map/ppermute | solution.py:36
  131.4 7.5 %collective-permute-start.30 = (bf16[136,256]{1,0:T(8,128)(2,1)S(1)}, bf16[136,256]{1,0:T(8,128)(2,1)S(1)}, u32[]{:S(2)}, u32[]{:S(2)}) collective-permute-start(bf16[136,256]{1,0:T(8,128)(2,1)S(1)} %get-tuple-element.24.refs_3_), channel_id=1, source_target_pairs={{32,256},{33,257},{34,258},{35,259},{36,260},{37,261},{38,262},{39... | collective-permute-start | bytes 208904 | tf_op jit(solution)/shard_map/ppermute | solution.py:36
  132.8 8.6 %collective-permute-start.24 = (bf16[1,136,256]{2,1,0:T(8,128)(2,1)S(1)}, bf16[1,136,256]{2,1,0:T(8,128)(2,1)S(1)}, u32[]{:S(2)}, u32[]{:S(2)}) collective-permute-start(bf16[1,136,256]{2,1,0:T(8,128)(2,1)S(1)} %select_bitcast_fusion.3), channel_id=1, source_target_pairs={{0,16},{1,17},{2,18},{3,19},{4,20},{5,21},{6,22},{7,23},{8,24},{9,... | collective-permute-start | bytes 208904 | tf_op jit(solution)/shard_map/ppermute | solution.py:27
  138.9 10.7 %collective-permute-start.31 = (bf16[136,256]{1,0:T(8,128)(2,1)S(1)}, bf16[136,256]{1,0:T(8,128)(2,1)S(1)}, u32[]{:S(2)}, u32[]{:S(2)}) collective-permute-start(bf16[136,256]{1,0:T(8,128)(2,1)S(1)} %collective-permute-done.30), channel_id=1, source_target_pairs={{32,0},{33,1},{34,2},{35,3},{36,4},{37,5},{38,6},{39,7},{40,8},{41... | collective-permute-start | bytes 208904 | tf_op jit(solution)/shard_map/ppermute | solution.py:36
  141.3 11.0 %collective-permute-start.25 = (bf16[2,136,256]{2,1,0:T(8,128)(2,1)S(1)}, bf16[2,136,256]{2,1,0:T(8,128)(2,1)S(1)}, u32[]{:S(2)}, u32[]{:S(2)}) collective-permute-start(bf16[2,136,256]{2,1,0:T(8,128)(2,1)S(1)} %pad_maximum_fusion.5), channel_id=1, source_target_pairs={{0,8},{1,9},{2,10},{3,11},{4,12},{5,13},{6,14},{7,15},{8,0},{9,1},... | collective-permute-start | bytes 417800 | tf_op jit(solution)/shard_map/ppermute | solution.py:27
  149.6 6.0 %collective-permute-start.32 = (bf16[1,136,256]{2,1,0:T(8,128)(2,1)S(1)}, bf16[1,136,256]{2,1,0:T(8,128)(2,1)S(1)}, u32[]{:S(2)}, u32[]{:S(2)}) collective-permute-start(bf16[1,136,256]{2,1,0:T(8,128)(2,1)S(1)} %select_bitcast_fusion.2), channel_id=1, source_target_pairs={{0,16},{1,17},{2,18},{3,19},{4,20},{5,21},{6,22},{7,23},{8,24},{9,... | collective-permute-start | bytes 208904 | tf_op jit(solution)/shard_map/ppermute | solution.py:27
  152.4 17.8 %collective-permute-start.26 = (bf16[4,136,256]{2,1,0:T(8,128)(2,1)S(1)}, bf16[4,136,256]{2,1,0:T(8,128)(2,1)S(1)}, u32[]{:S(2)}, u32[]{:S(2)}) collective-permute-start(bf16[4,136,256]{2,1,0:T(8,128)(2,1)S(1)} %pad_maximum_fusion.2.refs_0_), channel_id=1, source_target_pairs={{0,2},{1,3},{2,0},{3,1},{4,6},{5,7},{6,4},{7,5},{8,10},{9,11},{10,... | collective-permute-start | bytes 835592 | tf_op jit(solution)/shard_map/ppermute | solution.py:27
  155.6 9.3 %collective-permute-start.34 = (bf16[2,136,256]{2,1,0:T(8,128)(2,1)S(1)}, bf16[2,136,256]{2,1,0:T(8,128)(2,1)S(1)}, u32[]{:S(2)}, u32[]{:S(2)}) collective-permute-start(bf16[2,136,256]{2,1,0:T(8,128)(2,1)S(1)} %pad_maximum_fusion.6.refs_0_), channel_id=1, source_target_pairs={{0,6},{1,7},{2,4},{3,5},{4,2},{5,3},{6,0},{7,1},{8,14},{9,15},{10,... | collective-permute-start | bytes 417800 | tf_op jit(solution)/shard_map/ppermute | solution.py:27
  158.5 16.3 %collective-permute-start.36 = (bf16[2,136,256]{2,1,0:T(8,128)(2,1)S(1)}, bf16[2,136,256]{2,1,0:T(8,128)(2,1)S(1)}, u32[]{:S(2)}, u32[]{:S(2)}) collective-permute-start(bf16[2,136,256]{2,1,0:T(8,128)(2,1)S(1)} %pad_maximum_fusion.6.refs_0_), channel_id=1, source_target_pairs={{0,8},{1,9},{2,10},{3,11},{4,12},{5,13},{6,14},{7,15},{8,0},{9,1},... | collective-permute-start | bytes 417800 | tf_op jit(solution)/shard_map/ppermute | solution.py:27
  163.0 13.8 %collective-permute-start.33 = (bf16[2,136,256]{2,1,0:T(8,128)(2,1)S(1)}, bf16[2,136,256]{2,1,0:T(8,128)(2,1)S(1)}, u32[]{:S(2)}, u32[]{:S(2)}) collective-permute-start(bf16[2,136,256]{2,1,0:T(8,128)(2,1)S(1)} %pad_maximum_fusion.6.refs_0_), channel_id=1, source_target_pairs={{0,2},{1,3},{2,0},{3,1},{4,6},{5,7},{6,4},{7,5},{8,10},{9,11},{10,... | collective-permute-start | bytes 417800 | tf_op jit(solution)/shard_map/ppermute | solution.py:27
  164.9 14.9 %collective-permute-start.35 = (bf16[2,136,256]{2,1,0:T(8,128)(2,1)S(1)}, bf16[2,136,256]{2,1,0:T(8,128)(2,1)S(1)}, u32[]{:S(2)}, u32[]{:S(2)}) collective-permute-start(bf16[2,136,256]{2,1,0:T(8,128)(2,1)S(1)} %collective-permute-done.34.refs_3_), channel_id=1, source_target_pairs={{0,2},{1,3},{2,0},{3,1},{4,6},{5,7},{6,4},{7,5},{8,10},{9,11},{10,... | collective-permute-start | bytes 417800 | tf_op jit(solution)/shard_map/ppermute | solution.py:27
  168.3 30.8 %collective-permute-start.28 = (bf16[4,136,256]{2,1,0:T(8,128)(2,1)S(1)}, bf16[4,136,256]{2,1,0:T(8,128)(2,1)S(1)}, u32[]{:S(2)}, u32[]{:S(2)}) collective-permute-start(bf16[4,136,256]{2,1,0:T(8,128)(2,1)S(1)} %pad_maximum_fusion.2.refs_0_), channel_id=1, source_target_pairs={{0,6},{1,7},{2,4},{3,5},{4,2},{5,3},{6,0},{7,1},{8,14},{9,15},{10,... | collective-permute-start | bytes 835592 | tf_op jit(solution)/shard_map/ppermute | solution.py:27
  170.2 28.9 %collective-permute-start.27 = (bf16[4,136,256]{2,1,0:T(8,128)(2,1)S(1)}, bf16[4,136,256]{2,1,0:T(8,128)(2,1)S(1)}, u32[]{:S(2)}, u32[]{:S(2)}) collective-permute-start(bf16[4,136,256]{2,1,0:T(8,128)(2,1)S(1)} %collective-permute-done.26.refs_1_), channel_id=1, source_target_pairs={{0,6},{1,7},{2,4},{3,5},{4,2},{5,3},{6,0},{7,1},{8,14},{9,15},{10,... | collective-permute-start | bytes 835592 | tf_op jit(solution)/shard_map/ppermute | solution.py:27
  174.8 9.6 %collective-permute-start.37 = (bf16[2,136,256]{2,1,0:T(8,128)(2,1)S(1)}, bf16[2,136,256]{2,1,0:T(8,128)(2,1)S(1)}, u32[]{:S(2)}, u32[]{:S(2)}) collective-permute-start(bf16[2,136,256]{2,1,0:T(8,128)(2,1)S(1)} %collective-permute-done.36.refs_4_), channel_id=1, source_target_pairs={{0,2},{1,3},{2,0},{3,1},{4,6},{5,7},{6,4},{7,5},{8,10},{9,11},{10,... | collective-permute-start | bytes 417800 | tf_op jit(solution)/shard_map/ppermute | solution.py:27
  176.8 7.7 %collective-permute-start.38 = (bf16[2,136,256]{2,1,0:T(8,128)(2,1)S(1)}, bf16[2,136,256]{2,1,0:T(8,128)(2,1)S(1)}, u32[]{:S(2)}, u32[]{:S(2)}) collective-permute-start(bf16[2,136,256]{2,1,0:T(8,128)(2,1)S(1)} %collective-permute-done.36.refs_4_), channel_id=1, source_target_pairs={{0,4},{1,5},{2,6},{3,7},{4,0},{5,1},{6,2},{7,3},{8,12},{9,13},{10,... | collective-permute-start | bytes 417800 | tf_op jit(solution)/shard_map/ppermute | solution.py:27
  179.9 8.8 %collective-permute-start.39 = (bf16[2,136,256]{2,1,0:T(8,128)(2,1)S(1)}, bf16[2,136,256]{2,1,0:T(8,128)(2,1)S(1)}, u32[]{:S(2)}, u32[]{:S(2)}) collective-permute-start(bf16[2,136,256]{2,1,0:T(8,128)(2,1)S(1)} %collective-permute-done.36.refs_4_), channel_id=1, source_target_pairs={{0,6},{1,7},{2,4},{3,5},{4,2},{5,3},{6,0},{7,1},{8,14},{9,15},{10,... | collective-permute-start | bytes 417800 | tf_op jit(solution)/shard_map/ppermute | solution.py:27
  190.7 12.4 %collective-permute-start.40 = (f32[136,256]{1,0:T(8,128)S(1)}, f32[136,256]{1,0:T(8,128)S(1)}, u32[]{:S(2)}, u32[]{:S(2)}) collective-permute-start(f32[136,256]{1,0:T(8,128)S(1)} %get-tuple-element.28), channel_id=1, source_target_pairs={{0,1},{1,0},{2,3},{3,2},{4,5},{5,4},{6,7},{7,6},{8,9},{9,8},{10,11... | collective-permute-start | bytes 417800 | tf_op jit(solution)/shard_map/ppermute | solution.py:27
  201.2 19.0 %collective-permute-start.29 = (f32[136,256]{1,0:T(8,128)S(1)}, f32[136,256]{1,0:T(8,128)S(1)}, u32[]{:S(2)}, u32[]{:S(2)}) collective-permute-start(f32[136,256]{1,0:T(8,128)S(1)} %get-tuple-element.26), channel_id=1, source_target_pairs={{0,1},{1,0},{2,3},{3,2},{4,5},{5,4},{6,7},{7,6},{8,9},{9,8},{10,11... | collective-permute-start | bytes 417800 | tf_op jit(solution)/shard_map/ppermute | solution.py:27
  203.2 17.0 %collective-permute-start.41 = (bf16[136,256]{1,0:T(8,128)(2,1)S(1)}, bf16[136,256]{1,0:T(8,128)(2,1)S(1)}, u32[]{:S(2)}, u32[]{:S(2)}) collective-permute-start(bf16[136,256]{1,0:T(8,128)(2,1)S(1)} %fold.3), channel_id=1, source_target_pairs={{0,256},{1,257},{2,258},{3,259},{4,260},{5,261},{6,262},{7,263},{8... | collective-permute-start | bytes 208904 | tf_op jit(solution)/shard_map/ppermute | solution.py:27
  (12 other events, 141.0 us)
where the time goes:
time: 223 us; the launch traced here: 221 us
  starting transfers between devices  141 us (63%)
  waiting for transfers between devices  61.5 us (28%)
  Pallas kernels  10.2 us (5%)
  other arithmetic  3.6 us (2%)
  local copies, waits for them, and re-layouts  3.41 us (2%)
    ppermute x36, starting transfers between devices, permute(): return lax.ppermute(value, AXES, pairs)  118 us
    ppermute x36, waiting for transfers between devices, permute(): return lax.ppermute(value, AXES, pairs)  45.9 us
    ppermute x6, starting transfers between devices, some(): return lax.ppermute(value, AXES, pairs)  23 us
    ppermute x6, waiting for transfers between devices, some(): return lax.ppermute(value, AXES, pairs)  15.6 us
    pallas_call x4, Pallas kernels, mix(): pl.pallas_call(functools.partial(mix_kernel, pieces=len(spikes) // 4, row...  8.08 us
  transfers between devices with their start and end apart: 42, of which 13 were waited for; matrix products, arithmetic and copies ran while one was open for 2% of the time, Pallas kernels for 4%

commit v1 on v0

--- a/solution.py
+++ b/solution.py
@@ -326,14 +326,14 @@
         if step == 0:
             half[0], place, lanes = lax.optimization_barrier((half[0], place, lanes))
         last = [over_b(half[0], 1)]
-        for pieces, near, far in ((keep, 1, 3), (half, 3, 1)):
-            came = {}
-            for k in (near, far):
-                came[k] = over_y(pieces[0], k)
-            came[2] = over_y(came[near], far)
-            pieces += [came[k] for k in (1, 2, 3)]
-        for k in (1, 2, 3):
-            last.append(over_y(last[0], k))
+        came = {}
+        for k in (3, 1):
+            came[k] = over_y(half[0], k)
+        came[2] = over_y(came[3], 1)
+        half += [came[k] for k in (1, 2, 3)]
+        for pieces in (last, keep):
+            for k in (1, 2, 3):
+                pieces.append(over_y(pieces[0], k))
         mine, theirs = mix(place, half + last, weights, rows, trials)
         theirs = over_c(theirs)
         give = fold(mine, theirs, rows, trials)

time: 223 us -> 217 us (0.973)
  the two profiles are of different devices: /device:TPU:1 before, /device:TPU:35 now
where the time goes in v1:
time: 217 us; the launch traced here: 216 us
  starting transfers between devices  172 us (79%)
  waiting for transfers between devices  32.4 us (15%)
  Pallas kernels  7.41 us (3%)
    ppermute x36, starting transfers between devices, permute(): return lax.ppermute(value, AXES, pairs)  136 us
    ppermute x6, starting transfers between devices, some(): return lax.ppermute(value, AXES, pairs)  35.9 us
    ppermute x36, waiting for transfers between devices, permute(): return lax.ppermute(value, AXES, pairs)  32.4 us
    pallas_call x4, Pallas kernels, mix(): pl.pallas_call(functools.partial(mix_kernel, pieces=len(spikes) // 4, row...  5.31 us
  transfers between devices with their start and end apart: 42, of which 10 were waited for; matrix products, arithmetic and copies ran while one was open for 0% of the time, Pallas kernels for 3%

profile of v1, /device:TPU:35, one launch (start us, length us, event | category | flops | bytes accessed | tf_op | source)
XLA Modules:
  0.0 215.6 jit_solution(2778595254580200468)
XLA Ops:
  0.6 1.5 copy.16
  2.4 2.7 %collective-permute-start.9 = (bf16[4,256,256]{2,1,0:T(8,128)(2,1)S(1)}, bf16[4,256,256]{2,1,0:T(8,128)(2,1)S(1)}, u32[]{:S(2)}, u32[]{:S(2)}) collective-permute-start(bf16[4,256,256]{2,1,0:T(8,128)(2,1)S(1)} %get-tuple-element.33), channel_id=1, source_target_pairs={{0,1},{1,0},{2,3},{3,2},{4,5},{5,4},{6,7},{7,6},{8,9},{9,8},{10,11... | collective-permute-start | bytes 1572872 | tf_op jit(solution)/shard_map/ppermute | solution.py:27
  6.0 16.1 %collective-permute-start.3 = (bf16[136,256]{1,0:T(8,128)(2,1)S(1)}, bf16[136,256]{1,0:T(8,128)(2,1)S(1)}, u32[]{:S(2)}, u32[]{:S(2)}) collective-permute-start(bf16[136,256]{1,0:T(8,128)(2,1)S(1)} %pack.1.refs_3_), channel_id=1, source_target_pairs={{0,32},{1,33},{2,34},{3,35},{4,36},{5,37},{6,38},{7,39},{8,40},{9,... | collective-permute-start | bytes 208904 | tf_op jit(solution)/shard_map/ppermute | solution.py:36
  23.8 2.2 %collective-permute-start.10 = (bf16[4,256,512]{2,1,0:T(8,128)(2,1)S(1)}, bf16[4,256,512]{2,1,0:T(8,128)(2,1)S(1)}, u32[]{:S(2)}, u32[]{:S(2)}) collective-permute-start(bf16[4,256,512]{2,1,0:T(8,128)(2,1)S(1)} %pad_maximum_fusion.refs_4_.refs_8_), channel_id=1, source_target_pairs={{0,64},{1,65},{2,66},{3,67},{4,68},{5,69},{6,70},{7,71},{8,72},{9,... | collective-permute-start | bytes 3145736 | tf_op jit(solution)/shard_map/ppermute | solution.py:27
  26.0 3.1 %collective-permute-start.4 = (bf16[1,136,256]{2,1,0:T(8,128)(2,1)S(1)}, bf16[1,136,256]{2,1,0:T(8,128)(2,1)S(1)}, u32[]{:S(2)}, u32[]{:S(2)}) collective-permute-start(bf16[1,136,256]{2,1,0:T(8,128)(2,1)S(1)} %select_bitcast_fusion.4), channel_id=1, source_target_pairs={{0,16},{1,17},{2,18},{3,19},{4,20},{5,21},{6,22},{7,23},{8,24},{9,... | collective-permute-start | bytes 208904 | tf_op jit(solution)/shard_map/ppermute | solution.py:27
  29.2 4.1 %collective-permute-start.11 = (bf16[4,256,512]{2,1,0:T(8,128)(2,1)S(1)}, bf16[4,256,512]{2,1,0:T(8,128)(2,1)S(1)}, u32[]{:S(2)}, u32[]{:S(2)}) collective-permute-start(bf16[4,256,512]{2,1,0:T(8,128)(2,1)S(1)} %pad_maximum_fusion.refs_4_.refs_8_), channel_id=1, source_target_pairs={{0,128},{1,129},{2,130},{3,131},{4,132},{5,133},{6,134},{7,135},{8... | collective-permute-start | bytes 3145736 | tf_op jit(solution)/shard_map/ppermute | solution.py:27
  33.2 2.2 %collective-permute-start.12 = (bf16[4,256,512]{2,1,0:T(8,128)(2,1)S(1)}, bf16[4,256,512]{2,1,0:T(8,128)(2,1)S(1)}, u32[]{:S(2)}, u32[]{:S(2)}) collective-permute-start(bf16[4,256,512]{2,1,0:T(8,128)(2,1)S(1)} %pad_maximum_fusion.refs_4_.refs_8_), channel_id=1, source_target_pairs={{0,192},{1,193},{2,194},{3,195},{4,196},{5,197},{6,198},{7,199},{8... | collective-permute-start | bytes 3145736 | tf_op jit(solution)/shard_map/ppermute | solution.py:27
  35.4 3.1 %collective-permute-start.2 = (bf16[1,136,256]{2,1,0:T(8,128)(2,1)S(1)}, bf16[1,136,256]{2,1,0:T(8,128)(2,1)S(1)}, u32[]{:S(2)}, u32[]{:S(2)}) collective-permute-start(bf16[1,136,256]{2,1,0:T(8,128)(2,1)S(1)} %select_bitcast_fusion.5), channel_id=1, source_target_pairs={{0,16},{1,17},{2,18},{3,19},{4,20},{5,21},{6,22},{7,23},{8,24},{9,... | collective-permute-start | bytes 208904 | tf_op jit(solution)/shard_map/ppermute | solution.py:27
  38.5 2.6 %collective-permute-start.5 = (bf16[2,136,256]{2,1,0:T(8,128)(2,1)S(1)}, bf16[2,136,256]{2,1,0:T(8,128)(2,1)S(1)}, u32[]{:S(2)}, u32[]{:S(2)}) collective-permute-start(bf16[2,136,256]{2,1,0:T(8,128)(2,1)S(1)} %pad_maximum_fusion.4), channel_id=1, source_target_pairs={{0,8},{1,9},{2,10},{3,11},{4,12},{5,13},{6,14},{7,15},{8,0},{9,1},... | collective-permute-start | bytes 417800 | tf_op jit(solution)/shard_map/ppermute | solution.py:27
  41.4 3.8 %collective-permute-start.17 = (bf16[2,136,256]{2,1,0:T(8,128)(2,1)S(1)}, bf16[2,136,256]{2,1,0:T(8,128)(2,1)S(1)}, u32[]{:S(2)}, u32[]{:S(2)}) collective-permute-start(bf16[2,136,256]{2,1,0:T(8,128)(2,1)S(1)} %pad_maximum_fusion.3.refs_0_), channel_id=1, source_target_pairs={{0,8},{1,9},{2,10},{3,11},{4,12},{5,13},{6,14},{7,15},{8,0},{9,1},... | collective-permute-start | bytes 417800 | tf_op jit(solution)/shard_map/ppermute | solution.py:27
  45.2 4.6 %collective-permute-start.15 = (bf16[2,136,256]{2,1,0:T(8,128)(2,1)S(1)}, bf16[2,136,256]{2,1,0:T(8,128)(2,1)S(1)}, u32[]{:S(2)}, u32[]{:S(2)}) collective-permute-start(bf16[2,136,256]{2,1,0:T(8,128)(2,1)S(1)} %pad_maximum_fusion.3.refs_0_), channel_id=1, source_target_pairs={{0,6},{1,7},{2,4},{3,5},{4,2},{5,3},{6,0},{7,1},{8,14},{9,15},{10,... | collective-permute-start | bytes 417800 | tf_op jit(solution)/shard_map/ppermute | solution.py:27
  49.9 1.9 collective-permute-start.14
  52.3 2.9 %collective-permute-start.18 = (bf16[2,136,256]{2,1,0:T(8,128)(2,1)S(1)}, bf16[2,136,256]{2,1,0:T(8,128)(2,1)S(1)}, u32[]{:S(2)}, u32[]{:S(2)}) collective-permute-start(bf16[2,136,256]{2,1,0:T(8,128)(2,1)S(1)} %collective-permute-done.17.refs_4_), channel_id=1, source_target_pairs={{0,2},{1,3},{2,0},{3,1},{4,6},{5,7},{6,4},{7,5},{8,10},{9,11},{10,... | collective-permute-start | bytes 417800 | tf_op jit(solution)/shard_map/ppermute | solution.py:27
  56.0 4.0 %collective-permute-start.19 = (bf16[2,136,256]{2,1,0:T(8,128)(2,1)S(1)}, bf16[2,136,256]{2,1,0:T(8,128)(2,1)S(1)}, u32[]{:S(2)}, u32[]{:S(2)}) collective-permute-start(bf16[2,136,256]{2,1,0:T(8,128)(2,1)S(1)} %collective-permute-done.17.refs_4_), channel_id=1, source_target_pairs={{0,4},{1,5},{2,6},{3,7},{4,0},{5,1},{6,2},{7,3},{8,12},{9,13},{10,... | collective-permute-start | bytes 417800 | tf_op jit(solution)/shard_map/ppermute | solution.py:27
  60.0 3.3 %collective-permute-start.20 = (bf16[2,136,256]{2,1,0:T(8,128)(2,1)S(1)}, bf16[2,136,256]{2,1,0:T(8,128)(2,1)S(1)}, u32[]{:S(2)}, u32[]{:S(2)}) collective-permute-start(bf16[2,136,256]{2,1,0:T(8,128)(2,1)S(1)} %collective-permute-done.17.refs_4_), channel_id=1, source_target_pairs={{0,6},{1,7},{2,4},{3,5},{4,2},{5,3},{6,0},{7,1},{8,14},{9,15},{10,... | collective-permute-start | bytes 417800 | tf_op jit(solution)/shard_map/ppermute | solution.py:27
  63.5 2.0 collective-permute-start.16
  65.6 3.1 %collective-permute-done.20.refs_7_ = bf16[2,136,256]{2,1,0:T(8,128)(2,1)S(1)} collective-permute-done((bf16[2,136,256]{2,1,0:T(8,128)(2,1)S(1)}, bf16[2,136,256]{2,1,0:T(8,128)(2,1)S(1)}, u32[]{:S(2)}, u32[]{:S(2)}) %collective-permute-start.20) | collective-permute-done | bytes 139296 | tf_op jit(solution)/shard_map/ppermute | solution.py:27
  68.6 1.9 collective-permute-start.6
  70.6 3.6 %collective-permute-start.7 = (bf16[4,136,256]{2,1,0:T(8,128)(2,1)S(1)}, bf16[4,136,256]{2,1,0:T(8,128)(2,1)S(1)}, u32[]{:S(2)}, u32[]{:S(2)}) collective-permute-start(bf16[4,136,256]{2,1,0:T(8,128)(2,1)S(1)} %pad_maximum_fusion.1.refs_0_), channel_id=1, source_target_pairs={{0,4},{1,5},{2,6},{3,7},{4,0},{5,1},{6,2},{7,3},{8,12},{9,13},{10,... | collective-permute-start | bytes 835592 | tf_op jit(solution)/shard_map/ppermute | solution.py:27
  74.2 4.1 %collective-permute-start.8 = (bf16[4,136,256]{2,1,0:T(8,128)(2,1)S(1)}, bf16[4,136,256]{2,1,0:T(8,128)(2,1)S(1)}, u32[]{:S(2)}, u32[]{:S(2)}) collective-permute-start(bf16[4,136,256]{2,1,0:T(8,128)(2,1)S(1)} %pad_maximum_fusion.1.refs_0_), channel_id=1, source_target_pairs={{0,6},{1,7},{2,4},{3,5},{4,2},{5,3},{6,0},{7,1},{8,14},{9,15},{10,... | collective-permute-start | bytes 835592 | tf_op jit(solution)/shard_map/ppermute | solution.py:27
  79.1 1.3 shard_map.150
  80.5 7.9 %collective-permute-start.21 = (f32[136,256]{1,0:T(8,128)S(1)}, f32[136,256]{1,0:T(8,128)S(1)}, u32[]{:S(2)}, u32[]{:S(2)}) collective-permute-start(f32[136,256]{1,0:T(8,128)S(1)} %get-tuple-element.22), channel_id=1, source_target_pairs={{0,1},{1,0},{2,3},{3,2},{4,5},{5,4},{6,7},{7,6},{8,9},{9,8},{10,11... | collective-permute-start | bytes 417800 | tf_op jit(solution)/shard_map/ppermute | solution.py:27
  88.4 1.3 shard_map.149
  89.8 5.0 %collective-permute-start.13 = (f32[136,256]{1,0:T(8,128)S(1)}, f32[136,256]{1,0:T(8,128)S(1)}, u32[]{:S(2)}, u32[]{:S(2)}) collective-permute-start(f32[136,256]{1,0:T(8,128)S(1)} %get-tuple-element.19), channel_id=1, source_target_pairs={{0,1},{1,0},{2,3},{3,2},{4,5},{5,4},{6,7},{7,6},{8,9},{9,8},{10,11... | collective-permute-start | bytes 417800 | tf_op jit(solution)/shard_map/ppermute | solution.py:27
  94.8 12.3 %collective-permute-start.22 = (bf16[136,256]{1,0:T(8,128)(2,1)S(1)}, bf16[136,256]{1,0:T(8,128)(2,1)S(1)}, u32[]{:S(2)}, u32[]{:S(2)}) collective-permute-start(bf16[136,256]{1,0:T(8,128)(2,1)S(1)} %fold.2), channel_id=1, source_target_pairs={{0,256},{1,257},{2,258},{3,259},{4,260},{5,261},{6,262},{7,263},{8... | collective-permute-start | bytes 208904 | tf_op jit(solution)/shard_map/ppermute | solution.py:27
  107.2 2.5 %collective-permute-done.22.refs_2_ = bf16[136,256]{1,0:T(8,128)(2,1)S(1)} collective-permute-done((bf16[136,256]{1,0:T(8,128)(2,1)S(1)}, bf16[136,256]{1,0:T(8,128)(2,1)S(1)}, u32[]{:S(2)}, u32[]{:S(2)}) %collective-permute-start.22) | collective-permute-done | bytes 69664 | tf_op jit(solution)/shard_map/ppermute | solution.py:27
  112.6 15.9 %collective-permute-start.23 = (bf16[136,256]{1,0:T(8,128)(2,1)S(1)}, bf16[136,256]{1,0:T(8,128)(2,1)S(1)}, u32[]{:S(2)}, u32[]{:S(2)}) collective-permute-start(bf16[136,256]{1,0:T(8,128)(2,1)S(1)} %get-tuple-element.24.refs_3_), channel_id=1, source_target_pairs={{0,32},{1,33},{2,34},{3,35},{4,36},{5,37},{6,38},{7,39},{8,40},{9,... | collective-permute-start | bytes 208904 | tf_op jit(solution)/shard_map/ppermute | solution.py:36
  128.5 7.2 %collective-permute-start.32 = (bf16[1,136,256]{2,1,0:T(8,128)(2,1)S(1)}, bf16[1,136,256]{2,1,0:T(8,128)(2,1)S(1)}, u32[]{:S(2)}, u32[]{:S(2)}) collective-permute-start(bf16[1,136,256]{2,1,0:T(8,128)(2,1)S(1)} %select_bitcast_fusion.2), channel_id=1, source_target_pairs={{0,16},{1,17},{2,18},{3,19},{4,20},{5,21},{6,22},{7,23},{8,24},{9,... | collective-permute-start | bytes 208904 | tf_op jit(solution)/shard_map/ppermute | solution.py:27
  135.8 1.9 collective-permute-start.24
  137.7 4.1 %collective-permute-start.34 = (bf16[2,136,256]{2,1,0:T(8,128)(2,1)S(1)}, bf16[2,136,256]{2,1,0:T(8,128)(2,1)S(1)}, u32[]{:S(2)}, u32[]{:S(2)}) collective-permute-start(bf16[2,136,256]{2,1,0:T(8,128)(2,1)S(1)} %pad_maximum_fusion.6.refs_0_), channel_id=1, source_target_pairs={{0,6},{1,7},{2,4},{3,5},{4,2},{5,3},{6,0},{7,1},{8,14},{9,15},{10,... | collective-permute-start | bytes 417800 | tf_op jit(solution)/shard_map/ppermute | solution.py:27
  141.9 6.4 %collective-permute-start.36 = (bf16[2,136,256]{2,1,0:T(8,128)(2,1)S(1)}, bf16[2,136,256]{2,1,0:T(8,128)(2,1)S(1)}, u32[]{:S(2)}, u32[]{:S(2)}) collective-permute-start(bf16[2,136,256]{2,1,0:T(8,128)(2,1)S(1)} %pad_maximum_fusion.6.refs_0_), channel_id=1, source_target_pairs={{0,8},{1,9},{2,10},{3,11},{4,12},{5,13},{6,14},{7,15},{8,0},{9,1},... | collective-permute-start | bytes 417800 | tf_op jit(solution)/shard_map/ppermute | solution.py:27
  148.3 1.9 collective-permute-start.25
  150.3 1.9 collective-permute-start.33
  152.2 3.4 %collective-permute-start.35 = (bf16[2,136,256]{2,1,0:T(8,128)(2,1)S(1)}, bf16[2,136,256]{2,1,0:T(8,128)(2,1)S(1)}, u32[]{:S(2)}, u32[]{:S(2)}) collective-permute-start(bf16[2,136,256]{2,1,0:T(8,128)(2,1)S(1)} %collective-permute-done.34.refs_3_), channel_id=1, source_target_pairs={{0,2},{1,3},{2,0},{3,1},{4,6},{5,7},{6,4},{7,5},{8,10},{9,11},{10,... | collective-permute-start | bytes 417800 | tf_op jit(solution)/shard_map/ppermute | solution.py:27
  155.6 1.9 collective-permute-start.37
  157.6 3.4 %collective-permute-start.26 = (bf16[4,136,256]{2,1,0:T(8,128)(2,1)S(1)}, bf16[4,136,256]{2,1,0:T(8,128)(2,1)S(1)}, u32[]{:S(2)}, u32[]{:S(2)}) collective-permute-start(bf16[4,136,256]{2,1,0:T(8,128)(2,1)S(1)} %pad_maximum_fusion.2.refs_0_), channel_id=1, source_target_pairs={{0,2},{1,3},{2,0},{3,1},{4,6},{5,7},{6,4},{7,5},{8,10},{9,11},{10,... | collective-permute-start | bytes 835592 | tf_op jit(solution)/shard_map/ppermute | solution.py:27
  160.9 4.3 %collective-permute-start.27 = (bf16[4,136,256]{2,1,0:T(8,128)(2,1)S(1)}, bf16[4,136,256]{2,1,0:T(8,128)(2,1)S(1)}, u32[]{:S(2)}, u32[]{:S(2)}) collective-permute-start(bf16[4,136,256]{2,1,0:T(8,128)(2,1)S(1)} %pad_maximum_fusion.2.refs_0_), channel_id=1, source_target_pairs={{0,4},{1,5},{2,6},{3,7},{4,0},{5,1},{6,2},{7,3},{8,12},{9,13},{10,... | collective-permute-start | bytes 835592 | tf_op jit(solution)/shard_map/ppermute | solution.py:27
  165.2 2.2 %collective-permute-start.28 = (bf16[4,136,256]{2,1,0:T(8,128)(2,1)S(1)}, bf16[4,136,256]{2,1,0:T(8,128)(2,1)S(1)}, u32[]{:S(2)}, u32[]{:S(2)}) collective-permute-start(bf16[4,136,256]{2,1,0:T(8,128)(2,1)S(1)} %pad_maximum_fusion.2.refs_0_), channel_id=1, source_target_pairs={{0,6},{1,7},{2,4},{3,5},{4,2},{5,3},{6,0},{7,1},{8,14},{9,15},{10,... | collective-permute-start | bytes 835592 | tf_op jit(solution)/shard_map/ppermute | solution.py:27
  167.5 4.3 %collective-permute-start.38 = (bf16[2,136,256]{2,1,0:T(8,128)(2,1)S(1)}, bf16[2,136,256]{2,1,0:T(8,128)(2,1)S(1)}, u32[]{:S(2)}, u32[]{:S(2)}) collective-permute-start(bf16[2,136,256]{2,1,0:T(8,128)(2,1)S(1)} %collective-permute-done.36.refs_4_), channel_id=1, source_target_pairs={{0,4},{1,5},{2,6},{3,7},{4,0},{5,1},{6,2},{7,3},{8,12},{9,13},{10,... | collective-permute-start | bytes 417800 | tf_op jit(solution)/shard_map/ppermute | solution.py:27
  171.7 2.5 %collective-permute-start.39 = (bf16[2,136,256]{2,1,0:T(8,128)(2,1)S(1)}, bf16[2,136,256]{2,1,0:T(8,128)(2,1)S(1)}, u32[]{:S(2)}, u32[]{:S(2)}) collective-permute-start(bf16[2,136,256]{2,1,0:T(8,128)(2,1)S(1)} %collective-permute-done.36.refs_4_), channel_id=1, source_target_pairs={{0,6},{1,7},{2,4},{3,5},{4,2},{5,3},{6,0},{7,1},{8,14},{9,15},{10,... | collective-permute-start | bytes 417800 | tf_op jit(solution)/shard_map/ppermute | solution.py:27
  174.3 5.4 %collective-permute-done.38.refs_6_ = bf16[2,136,256]{2,1,0:T(8,128)(2,1)S(1)} collective-permute-done((bf16[2,136,256]{2,1,0:T(8,128)(2,1)S(1)}, bf16[2,136,256]{2,1,0:T(8,128)(2,1)S(1)}, u32[]{:S(2)}, u32[]{:S(2)}) %collective-permute-start.38) | collective-permute-done | bytes 139296 | tf_op jit(solution)/shard_map/ppermute | solution.py:27
  179.6 7.3 %collective-permute-done.39.refs_7_ = bf16[2,136,256]{2,1,0:T(8,128)(2,1)S(1)} collective-permute-done((bf16[2,136,256]{2,1,0:T(8,128)(2,1)S(1)}, bf16[2,136,256]{2,1,0:T(8,128)(2,1)S(1)}, u32[]{:S(2)}, u32[]{:S(2)}) %collective-permute-start.39) | collective-permute-done | bytes 139296 | tf_op jit(solution)/shard_map/ppermute | solution.py:27
  186.9 1.3 shard_map.152
  188.2 4.2 %collective-permute-start.40 = (f32[136,256]{1,0:T(8,128)S(1)}, f32[136,256]{1,0:T(8,128)S(1)}, u32[]{:S(2)}, u32[]{:S(2)}) collective-permute-start(f32[136,256]{1,0:T(8,128)S(1)} %get-tuple-element.28), channel_id=1, source_target_pairs={{0,1},{1,0},{2,3},{3,2},{4,5},{5,4},{6,7},{7,6},{8,9},{9,8},{10,11... | collective-permute-start | bytes 417800 | tf_op jit(solution)/shard_map/ppermute | solution.py:27
  192.4 1.3 shard_map.151
  193.8 1.9 collective-permute-start.29
  195.7 7.4 %collective-permute-start.41 = (bf16[136,256]{1,0:T(8,128)(2,1)S(1)}, bf16[136,256]{1,0:T(8,128)(2,1)S(1)}, u32[]{:S(2)}, u32[]{:S(2)}) collective-permute-start(bf16[136,256]{1,0:T(8,128)(2,1)S(1)} %fold.3), channel_id=1, source_target_pairs={{0,256},{1,257},{2,258},{3,259},{4,260},{5,261},{6,262},{7,263},{8... | collective-permute-start | bytes 208904 | tf_op jit(solution)/shard_map/ppermute | solution.py:27
  203.1 11.6 %collective-permute-done.41.refs_2_ = bf16[136,256]{1,0:T(8,128)(2,1)S(1)} collective-permute-done((bf16[136,256]{1,0:T(8,128)(2,1)S(1)}, bf16[136,256]{1,0:T(8,128)(2,1)S(1)}, u32[]{:S(2)}, u32[]{:S(2)}) %collective-permute-start.41) | collective-permute-done | bytes 69664 | tf_op jit(solution)/shard_map/ppermute | solution.py:27
  (89 shorter events, 9.3 us)
Async XLA Ops:
  0.6 21.5 %copy-start = (bf16[700,256]{1,0:T(8,128)(2,1)S(1)}, bf16[700,256]{1,0:T(8,128)(2,1)}, u32[]{:S(2)}) copy-start(bf16[700,256]{1,0:T(8,128)(2,1)} %param.20) | copy-start | bytes 1075204
  2.4 21.4 %collective-permute-start.9 = (bf16[4,256,256]{2,1,0:T(8,128)(2,1)S(1)}, bf16[4,256,256]{2,1,0:T(8,128)(2,1)S(1)}, u32[]{:S(2)}, u32[]{:S(2)}) collective-permute-start(bf16[4,256,256]{2,1,0:T(8,128)(2,1)S(1)} %get-tuple-element.33), channel_id=1, source_target_pairs={{0,1},{1,0},{2,3},{3,2},{4,5},{5,4},{6,7},{7,6},{8,9},{9,8},{10,11... | collective-permute-start | bytes 1572872 | tf_op jit(solution)/shard_map/ppermute | solution.py:27
  5.3 17.1 %collective-permute-start = (bf16[136,256]{1,0:T(8,128)(2,1)S(1)}, bf16[136,256]{1,0:T(8,128)(2,1)S(1)}, u32[]{:S(2)}, u32[]{:S(2)}) collective-permute-start(bf16[136,256]{1,0:T(8,128)(2,1)S(1)} %pack.1.refs_3_), channel_id=1, source_target_pairs={{32,256},{33,257},{34,258},{35,259},{36,260},{37,261},{38,262},{39... | collective-permute-start | bytes 208904 | tf_op jit(solution)/shard_map/ppermute | solution.py:36
  6.0 20.0 %collective-permute-start.3 = (bf16[136,256]{1,0:T(8,128)(2,1)S(1)}, bf16[136,256]{1,0:T(8,128)(2,1)S(1)}, u32[]{:S(2)}, u32[]{:S(2)}) collective-permute-start(bf16[136,256]{1,0:T(8,128)(2,1)S(1)} %pack.1.refs_3_), channel_id=1, source_target_pairs={{0,32},{1,33},{2,34},{3,35},{4,36},{5,37},{6,38},{7,39},{8,40},{9,... | collective-permute-start | bytes 208904 | tf_op jit(solution)/shard_map/ppermute | solution.py:36
  22.4 12.9 %collective-permute-start.1 = (bf16[136,256]{1,0:T(8,128)(2,1)S(1)}, bf16[136,256]{1,0:T(8,128)(2,1)S(1)}, u32[]{:S(2)}, u32[]{:S(2)}) collective-permute-start(bf16[136,256]{1,0:T(8,128)(2,1)S(1)} %collective-permute-done), channel_id=1, source_target_pairs={{32,0},{33,1},{34,2},{35,3},{36,4},{37,5},{38,6},{39,7},{40,8},{41... | collective-permute-start | bytes 208904 | tf_op jit(solution)/shard_map/ppermute | solution.py:36
  23.8 50.4 %collective-permute-start.10 = (bf16[4,256,512]{2,1,0:T(8,128)(2,1)S(1)}, bf16[4,256,512]{2,1,0:T(8,128)(2,1)S(1)}, u32[]{:S(2)}, u32[]{:S(2)}) collective-permute-start(bf16[4,256,512]{2,1,0:T(8,128)(2,1)S(1)} %pad_maximum_fusion.refs_4_.refs_8_), channel_id=1, source_target_pairs={{0,64},{1,65},{2,66},{3,67},{4,68},{5,69},{6,70},{7,71},{8,72},{9,... | collective-permute-start | bytes 3145736 | tf_op jit(solution)/shard_map/ppermute | solution.py:27
  26.0 12.5 %collective-permute-start.4 = (bf16[1,136,256]{2,1,0:T(8,128)(2,1)S(1)}, bf16[1,136,256]{2,1,0:T(8,128)(2,1)S(1)}, u32[]{:S(2)}, u32[]{:S(2)}) collective-permute-start(bf16[1,136,256]{2,1,0:T(8,128)(2,1)S(1)} %select_bitcast_fusion.4), channel_id=1, source_target_pairs={{0,16},{1,17},{2,18},{3,19},{4,20},{5,21},{6,22},{7,23},{8,24},{9,... | collective-permute-start | bytes 208904 | tf_op jit(solution)/shard_map/ppermute | solution.py:27
  29.2 49.1 %collective-permute-start.11 = (bf16[4,256,512]{2,1,0:T(8,128)(2,1)S(1)}, bf16[4,256,512]{2,1,0:T(8,128)(2,1)S(1)}, u32[]{:S(2)}, u32[]{:S(2)}) collective-permute-start(bf16[4,256,512]{2,1,0:T(8,128)(2,1)S(1)} %pad_maximum_fusion.refs_4_.refs_8_), channel_id=1, source_target_pairs={{0,128},{1,129},{2,130},{3,131},{4,132},{5,133},{6,134},{7,135},{8... | collective-permute-start | bytes 3145736 | tf_op jit(solution)/shard_map/ppermute | solution.py:27
  33.2 45.9 %collective-permute-start.12 = (bf16[4,256,512]{2,1,0:T(8,128)(2,1)S(1)}, bf16[4,256,512]{2,1,0:T(8,128)(2,1)S(1)}, u32[]{:S(2)}, u32[]{:S(2)}) collective-permute-start(bf16[4,256,512]{2,1,0:T(8,128)(2,1)S(1)} %pad_maximum_fusion.refs_4_.refs_8_), channel_id=1, source_target_pairs={{0,192},{1,193},{2,194},{3,195},{4,196},{5,197},{6,198},{7,199},{8... | collective-permute-start | bytes 3145736 | tf_op jit(solution)/shard_map/ppermute | solution.py:27
  35.4 6.0 %collective-permute-start.2 = (bf16[1,136,256]{2,1,0:T(8,128)(2,1)S(1)}, bf16[1,136,256]{2,1,0:T(8,128)(2,1)S(1)}, u32[]{:S(2)}, u32[]{:S(2)}) collective-permute-start(bf16[1,136,256]{2,1,0:T(8,128)(2,1)S(1)} %select_bitcast_fusion.5), channel_id=1, source_target_pairs={{0,16},{1,17},{2,18},{3,19},{4,20},{5,21},{6,22},{7,23},{8,24},{9,... | collective-permute-start | bytes 208904 | tf_op jit(solution)/shard_map/ppermute | solution.py:27
  38.5 6.7 %collective-permute-start.5 = (bf16[2,136,256]{2,1,0:T(8,128)(2,1)S(1)}, bf16[2,136,256]{2,1,0:T(8,128)(2,1)S(1)}, u32[]{:S(2)}, u32[]{:S(2)}) collective-permute-start(bf16[2,136,256]{2,1,0:T(8,128)(2,1)S(1)} %pad_maximum_fusion.4), channel_id=1, source_target_pairs={{0,8},{1,9},{2,10},{3,11},{4,12},{5,13},{6,14},{7,15},{8,0},{9,1},... | collective-permute-start | bytes 417800 | tf_op jit(solution)/shard_map/ppermute | solution.py:27
  41.4 8.5 %collective-permute-start.17 = (bf16[2,136,256]{2,1,0:T(8,128)(2,1)S(1)}, bf16[2,136,256]{2,1,0:T(8,128)(2,1)S(1)}, u32[]{:S(2)}, u32[]{:S(2)}) collective-permute-start(bf16[2,136,256]{2,1,0:T(8,128)(2,1)S(1)} %pad_maximum_fusion.3.refs_0_), channel_id=1, source_target_pairs={{0,8},{1,9},{2,10},{3,11},{4,12},{5,13},{6,14},{7,15},{8,0},{9,1},... | collective-permute-start | bytes 417800 | tf_op jit(solution)/shard_map/ppermute | solution.py:27
  45.2 7.1 %collective-permute-start.15 = (bf16[2,136,256]{2,1,0:T(8,128)(2,1)S(1)}, bf16[2,136,256]{2,1,0:T(8,128)(2,1)S(1)}, u32[]{:S(2)}, u32[]{:S(2)}) collective-permute-start(bf16[2,136,256]{2,1,0:T(8,128)(2,1)S(1)} %pad_maximum_fusion.3.refs_0_), channel_id=1, source_target_pairs={{0,6},{1,7},{2,4},{3,5},{4,2},{5,3},{6,0},{7,1},{8,14},{9,15},{10,... | collective-permute-start | bytes 417800 | tf_op jit(solution)/shard_map/ppermute | solution.py:27
  49.9 6.1 %collective-permute-start.14 = (bf16[2,136,256]{2,1,0:T(8,128)(2,1)S(1)}, bf16[2,136,256]{2,1,0:T(8,128)(2,1)S(1)}, u32[]{:S(2)}, u32[]{:S(2)}) collective-permute-start(bf16[2,136,256]{2,1,0:T(8,128)(2,1)S(1)} %pad_maximum_fusion.3.refs_0_), channel_id=1, source_target_pairs={{0,2},{1,3},{2,0},{3,1},{4,6},{5,7},{6,4},{7,5},{8,10},{9,11},{10,... | collective-permute-start | bytes 417800 | tf_op jit(solution)/shard_map/ppermute | solution.py:27
  52.3 7.7 %collective-permute-start.18 = (bf16[2,136,256]{2,1,0:T(8,128)(2,1)S(1)}, bf16[2,136,256]{2,1,0:T(8,128)(2,1)S(1)}, u32[]{:S(2)}, u32[]{:S(2)}) collective-permute-start(bf16[2,136,256]{2,1,0:T(8,128)(2,1)S(1)} %collective-permute-done.17.refs_4_), channel_id=1, source_target_pairs={{0,2},{1,3},{2,0},{3,1},{4,6},{5,7},{6,4},{7,5},{8,10},{9,11},{10,... | collective-permute-start | bytes 417800 | tf_op jit(solution)/shard_map/ppermute | solution.py:27
  56.0 7.5 %collective-permute-start.19 = (bf16[2,136,256]{2,1,0:T(8,128)(2,1)S(1)}, bf16[2,136,256]{2,1,0:T(8,128)(2,1)S(1)}, u32[]{:S(2)}, u32[]{:S(2)}) collective-permute-start(bf16[2,136,256]{2,1,0:T(8,128)(2,1)S(1)} %collective-permute-done.17.refs_4_), channel_id=1, source_target_pairs={{0,4},{1,5},{2,6},{3,7},{4,0},{5,1},{6,2},{7,3},{8,12},{9,13},{10,... | collective-permute-start | bytes 417800 | tf_op jit(solution)/shard_map/ppermute | solution.py:27
  60.0 8.6 %collective-permute-start.20 = (bf16[2,136,256]{2,1,0:T(8,128)(2,1)S(1)}, bf16[2,136,256]{2,1,0:T(8,128)(2,1)S(1)}, u32[]{:S(2)}, u32[]{:S(2)}) collective-permute-start(bf16[2,136,256]{2,1,0:T(8,128)(2,1)S(1)} %collective-permute-done.17.refs_4_), channel_id=1, source_target_pairs={{0,6},{1,7},{2,4},{3,5},{4,2},{5,3},{6,0},{7,1},{8,14},{9,15},{10,... | collective-permute-start | bytes 417800 | tf_op jit(solution)/shard_map/ppermute | solution.py:27
  63.5 7.0 %collective-permute-start.16 = (bf16[2,136,256]{2,1,0:T(8,128)(2,1)S(1)}, bf16[2,136,256]{2,1,0:T(8,128)(2,1)S(1)}, u32[]{:S(2)}, u32[]{:S(2)}) collective-permute-start(bf16[2,136,256]{2,1,0:T(8,128)(2,1)S(1)} %collective-permute-done.15.refs_3_), channel_id=1, source_target_pairs={{0,2},{1,3},{2,0},{3,1},{4,6},{5,7},{6,4},{7,5},{8,10},{9,11},{10,... | collective-permute-start | bytes 417800 | tf_op jit(solution)/shard_map/ppermute | solution.py:27
  68.6 19.8 %collective-permute-start.6 = (bf16[4,136,256]{2,1,0:T(8,128)(2,1)S(1)}, bf16[4,136,256]{2,1,0:T(8,128)(2,1)S(1)}, u32[]{:S(2)}, u32[]{:S(2)}) collective-permute-start(bf16[4,136,256]{2,1,0:T(8,128)(2,1)S(1)} %pad_maximum_fusion.1.refs_0_), channel_id=1, source_target_pairs={{0,2},{1,3},{2,0},{3,1},{4,6},{5,7},{6,4},{7,5},{8,10},{9,11},{10,... | collective-permute-start | bytes 835592 | tf_op jit(solution)/shard_map/ppermute | solution.py:27
  70.6 17.8 %collective-permute-start.7 = (bf16[4,136,256]{2,1,0:T(8,128)(2,1)S(1)}, bf16[4,136,256]{2,1,0:T(8,128)(2,1)S(1)}, u32[]{:S(2)}, u32[]{:S(2)}) collective-permute-start(bf16[4,136,256]{2,1,0:T(8,128)(2,1)S(1)} %pad_maximum_fusion.1.refs_0_), channel_id=1, source_target_pairs={{0,4},{1,5},{2,6},{3,7},{4,0},{5,1},{6,2},{7,3},{8,12},{9,13},{10,... | collective-permute-start | bytes 835592 | tf_op jit(solution)/shard_map/ppermute | solution.py:27
  74.2 14.2 %collective-permute-start.8 = (bf16[4,136,256]{2,1,0:T(8,128)(2,1)S(1)}, bf16[4,136,256]{2,1,0:T(8,128)(2,1)S(1)}, u32[]{:S(2)}, u32[]{:S(2)}) collective-permute-start(bf16[4,136,256]{2,1,0:T(8,128)(2,1)S(1)} %pad_maximum_fusion.1.refs_0_), channel_id=1, source_target_pairs={{0,6},{1,7},{2,4},{3,5},{4,2},{5,3},{6,0},{7,1},{8,14},{9,15},{10,... | collective-permute-start | bytes 835592 | tf_op jit(solution)/shard_map/ppermute | solution.py:27
  80.4 29.2 %copy-start.2 = (bf16[64,4,256]{2,1,0:T(4,128)(2,1)S(1)}, bf16[64,4,256]{2,1,0:T(4,128)(2,1)}, u32[]{:S(2)}) copy-start(bf16[64,4,256]{2,1,0:T(4,128)(2,1)} %refs_9_.3) | copy-start | bytes 393220
  80.4 29.2 %copy-start.3 = (f32[64,2,256]{2,1,0:T(2,128)S(1)}, f32[64,2,256]{2,1,0:T(2,128)}, u32[]{:S(2)}) copy-start(f32[64,2,256]{2,1,0:T(2,128)} %refs_4_.1) | copy-start | bytes 393220
  80.5 29.2 %copy-start.4 = (f32[64,2,256]{2,1,0:T(2,128)S(1)}, f32[64,2,256]{2,1,0:T(2,128)}, u32[]{:S(2)}) copy-start(f32[64,2,256]{2,1,0:T(2,128)} %refs_5_.1) | copy-start | bytes 393220
  80.5 29.2 %copy-start.6 = (s32[64,2]{0,1:T(2,128)S(1)}, s32[64,2]{0,1:T(2,128)}, u32[]{:S(2)}) copy-start(s32[64,2]{0,1:T(2,128)} %param.22) | copy-start | bytes 1540
  80.5 29.2 %copy-start.7 = (s32[64]{0:T(128)S(1)}, s32[64]{0:T(128)}, u32[]{:S(2)}) copy-start(s32[64]{0:T(128)} %param.23) | copy-start | bytes 772
  80.5 14.3 %collective-permute-start.21 = (f32[136,256]{1,0:T(8,128)S(1)}, f32[136,256]{1,0:T(8,128)S(1)}, u32[]{:S(2)}, u32[]{:S(2)}) collective-permute-start(f32[136,256]{1,0:T(8,128)S(1)} %get-tuple-element.22), channel_id=1, source_target_pairs={{0,1},{1,0},{2,3},{3,2},{4,5},{5,4},{6,7},{7,6},{8,9},{9,8},{10,11... | collective-permute-start | bytes 417800 | tf_op jit(solution)/shard_map/ppermute | solution.py:27
  89.8 17.4 %collective-permute-start.13 = (f32[136,256]{1,0:T(8,128)S(1)}, f32[136,256]{1,0:T(8,128)S(1)}, u32[]{:S(2)}, u32[]{:S(2)}) collective-permute-start(f32[136,256]{1,0:T(8,128)S(1)} %get-tuple-element.19), channel_id=1, source_target_pairs={{0,1},{1,0},{2,3},{3,2},{4,5},{5,4},{6,7},{7,6},{8,9},{9,8},{10,11... | collective-permute-start | bytes 417800 | tf_op jit(solution)/shard_map/ppermute | solution.py:27
  94.8 14.9 %collective-permute-start.22 = (bf16[136,256]{1,0:T(8,128)(2,1)S(1)}, bf16[136,256]{1,0:T(8,128)(2,1)S(1)}, u32[]{:S(2)}, u32[]{:S(2)}) collective-permute-start(bf16[136,256]{1,0:T(8,128)(2,1)S(1)} %fold.2), channel_id=1, source_target_pairs={{0,256},{1,257},{2,258},{3,259},{4,260},{5,261},{6,262},{7,263},{8... | collective-permute-start | bytes 208904 | tf_op jit(solution)/shard_map/ppermute | solution.py:27
  110.6 0.7 collective-permute-start.30
  111.3 17.2 %collective-permute-start.31 = (bf16[136,256]{1,0:T(8,128)(2,1)S(1)}, bf16[136,256]{1,0:T(8,128)(2,1)S(1)}, u32[]{:S(2)}, u32[]{:S(2)}) collective-permute-start(bf16[136,256]{1,0:T(8,128)(2,1)S(1)} %collective-permute-done.30), channel_id=1, source_target_pairs={{32,0},{33,1},{34,2},{35,3},{36,4},{37,5},{38,6},{39,7},{40,8},{41... | collective-permute-start | bytes 208904 | tf_op jit(solution)/shard_map/ppermute | solution.py:36
  112.6 23.1 %collective-permute-start.23 = (bf16[136,256]{1,0:T(8,128)(2,1)S(1)}, bf16[136,256]{1,0:T(8,128)(2,1)S(1)}, u32[]{:S(2)}, u32[]{:S(2)}) collective-permute-start(bf16[136,256]{1,0:T(8,128)(2,1)S(1)} %get-tuple-element.24.refs_3_), channel_id=1, source_target_pairs={{0,32},{1,33},{2,34},{3,35},{4,36},{5,37},{6,38},{7,39},{8,40},{9,... | collective-permute-start | bytes 208904 | tf_op jit(solution)/shard_map/ppermute | solution.py:36
  128.5 9.2 %collective-permute-start.32 = (bf16[1,136,256]{2,1,0:T(8,128)(2,1)S(1)}, bf16[1,136,256]{2,1,0:T(8,128)(2,1)S(1)}, u32[]{:S(2)}, u32[]{:S(2)}) collective-permute-start(bf16[1,136,256]{2,1,0:T(8,128)(2,1)S(1)} %select_bitcast_fusion.2), channel_id=1, source_target_pairs={{0,16},{1,17},{2,18},{3,19},{4,20},{5,21},{6,22},{7,23},{8,24},{9,... | collective-permute-start | bytes 208904 | tf_op jit(solution)/shard_map/ppermute | solution.py:27
  135.8 12.5 %collective-permute-start.24 = (bf16[1,136,256]{2,1,0:T(8,128)(2,1)S(1)}, bf16[1,136,256]{2,1,0:T(8,128)(2,1)S(1)}, u32[]{:S(2)}, u32[]{:S(2)}) collective-permute-start(bf16[1,136,256]{2,1,0:T(8,128)(2,1)S(1)} %select_bitcast_fusion.3), channel_id=1, source_target_pairs={{0,16},{1,17},{2,18},{3,19},{4,20},{5,21},{6,22},{7,23},{8,24},{9,... | collective-permute-start | bytes 208904 | tf_op jit(solution)/shard_map/ppermute | solution.py:27
  137.7 14.5 %collective-permute-start.34 = (bf16[2,136,256]{2,1,0:T(8,128)(2,1)S(1)}, bf16[2,136,256]{2,1,0:T(8,128)(2,1)S(1)}, u32[]{:S(2)}, u32[]{:S(2)}) collective-permute-start(bf16[2,136,256]{2,1,0:T(8,128)(2,1)S(1)} %pad_maximum_fusion.6.refs_0_), channel_id=1, source_target_pairs={{0,6},{1,7},{2,4},{3,5},{4,2},{5,3},{6,0},{7,1},{8,14},{9,15},{10,... | collective-permute-start | bytes 417800 | tf_op jit(solution)/shard_map/ppermute | solution.py:27
  141.9 13.7 %collective-permute-start.36 = (bf16[2,136,256]{2,1,0:T(8,128)(2,1)S(1)}, bf16[2,136,256]{2,1,0:T(8,128)(2,1)S(1)}, u32[]{:S(2)}, u32[]{:S(2)}) collective-permute-start(bf16[2,136,256]{2,1,0:T(8,128)(2,1)S(1)} %pad_maximum_fusion.6.refs_0_), channel_id=1, source_target_pairs={{0,8},{1,9},{2,10},{3,11},{4,12},{5,13},{6,14},{7,15},{8,0},{9,1},... | collective-permute-start | bytes 417800 | tf_op jit(solution)/shard_map/ppermute | solution.py:27
  148.3 9.2 %collective-permute-start.25 = (bf16[2,136,256]{2,1,0:T(8,128)(2,1)S(1)}, bf16[2,136,256]{2,1,0:T(8,128)(2,1)S(1)}, u32[]{:S(2)}, u32[]{:S(2)}) collective-permute-start(bf16[2,136,256]{2,1,0:T(8,128)(2,1)S(1)} %pad_maximum_fusion.5), channel_id=1, source_target_pairs={{0,8},{1,9},{2,10},{3,11},{4,12},{5,13},{6,14},{7,15},{8,0},{9,1},... | collective-permute-start | bytes 417800 | tf_op jit(solution)/shard_map/ppermute | solution.py:27
  150.3 15.0 %collective-permute-start.33 = (bf16[2,136,256]{2,1,0:T(8,128)(2,1)S(1)}, bf16[2,136,256]{2,1,0:T(8,128)(2,1)S(1)}, u32[]{:S(2)}, u32[]{:S(2)}) collective-permute-start(bf16[2,136,256]{2,1,0:T(8,128)(2,1)S(1)} %pad_maximum_fusion.6.refs_0_), channel_id=1, source_target_pairs={{0,2},{1,3},{2,0},{3,1},{4,6},{5,7},{6,4},{7,5},{8,10},{9,11},{10,... | collective-permute-start | bytes 417800 | tf_op jit(solution)/shard_map/ppermute | solution.py:27
  152.2 15.2 %collective-permute-start.35 = (bf16[2,136,256]{2,1,0:T(8,128)(2,1)S(1)}, bf16[2,136,256]{2,1,0:T(8,128)(2,1)S(1)}, u32[]{:S(2)}, u32[]{:S(2)}) collective-permute-start(bf16[2,136,256]{2,1,0:T(8,128)(2,1)S(1)} %collective-permute-done.34.refs_3_), channel_id=1, source_target_pairs={{0,2},{1,3},{2,0},{3,1},{4,6},{5,7},{6,4},{7,5},{8,10},{9,11},{10,... | collective-permute-start | bytes 417800 | tf_op jit(solution)/shard_map/ppermute | solution.py:27
  155.6 16.1 %collective-permute-start.37 = (bf16[2,136,256]{2,1,0:T(8,128)(2,1)S(1)}, bf16[2,136,256]{2,1,0:T(8,128)(2,1)S(1)}, u32[]{:S(2)}, u32[]{:S(2)}) collective-permute-start(bf16[2,136,256]{2,1,0:T(8,128)(2,1)S(1)} %collective-permute-done.36.refs_4_), channel_id=1, source_target_pairs={{0,2},{1,3},{2,0},{3,1},{4,6},{5,7},{6,4},{7,5},{8,10},{9,11},{10,... | collective-permute-start | bytes 417800 | tf_op jit(solution)/shard_map/ppermute | solution.py:27
  157.6 34.8 %collective-permute-start.26 = (bf16[4,136,256]{2,1,0:T(8,128)(2,1)S(1)}, bf16[4,136,256]{2,1,0:T(8,128)(2,1)S(1)}, u32[]{:S(2)}, u32[]{:S(2)}) collective-permute-start(bf16[4,136,256]{2,1,0:T(8,128)(2,1)S(1)} %pad_maximum_fusion.2.refs_0_), channel_id=1, source_target_pairs={{0,2},{1,3},{2,0},{3,1},{4,6},{5,7},{6,4},{7,5},{8,10},{9,11},{10,... | collective-permute-start | bytes 835592 | tf_op jit(solution)/shard_map/ppermute | solution.py:27
  160.9 31.5 %collective-permute-start.27 = (bf16[4,136,256]{2,1,0:T(8,128)(2,1)S(1)}, bf16[4,136,256]{2,1,0:T(8,128)(2,1)S(1)}, u32[]{:S(2)}, u32[]{:S(2)}) collective-permute-start(bf16[4,136,256]{2,1,0:T(8,128)(2,1)S(1)} %pad_maximum_fusion.2.refs_0_), channel_id=1, source_target_pairs={{0,4},{1,5},{2,6},{3,7},{4,0},{5,1},{6,2},{7,3},{8,12},{9,13},{10,... | collective-permute-start | bytes 835592 | tf_op jit(solution)/shard_map/ppermute | solution.py:27
  165.2 27.2 %collective-permute-start.28 = (bf16[4,136,256]{2,1,0:T(8,128)(2,1)S(1)}, bf16[4,136,256]{2,1,0:T(8,128)(2,1)S(1)}, u32[]{:S(2)}, u32[]{:S(2)}) collective-permute-start(bf16[4,136,256]{2,1,0:T(8,128)(2,1)S(1)} %pad_maximum_fusion.2.refs_0_), channel_id=1, source_target_pairs={{0,6},{1,7},{2,4},{3,5},{4,2},{5,3},{6,0},{7,1},{8,14},{9,15},{10,... | collective-permute-start | bytes 835592 | tf_op jit(solution)/shard_map/ppermute | solution.py:27
  167.5 12.2 %collective-permute-start.38 = (bf16[2,136,256]{2,1,0:T(8,128)(2,1)S(1)}, bf16[2,136,256]{2,1,0:T(8,128)(2,1)S(1)}, u32[]{:S(2)}, u32[]{:S(2)}) collective-permute-start(bf16[2,136,256]{2,1,0:T(8,128)(2,1)S(1)} %collective-permute-done.36.refs_4_), channel_id=1, source_target_pairs={{0,4},{1,5},{2,6},{3,7},{4,0},{5,1},{6,2},{7,3},{8,12},{9,13},{10,... | collective-permute-start | bytes 417800 | tf_op jit(solution)/shard_map/ppermute | solution.py:27
  171.7 15.2 %collective-permute-start.39 = (bf16[2,136,256]{2,1,0:T(8,128)(2,1)S(1)}, bf16[2,136,256]{2,1,0:T(8,128)(2,1)S(1)}, u32[]{:S(2)}, u32[]{:S(2)}) collective-permute-start(bf16[2,136,256]{2,1,0:T(8,128)(2,1)S(1)} %collective-permute-done.36.refs_4_), channel_id=1, source_target_pairs={{0,6},{1,7},{2,4},{3,5},{4,2},{5,3},{6,0},{7,1},{8,14},{9,15},{10,... | collective-permute-start | bytes 417800 | tf_op jit(solution)/shard_map/ppermute | solution.py:27
  188.2 7.5 %collective-permute-start.40 = (f32[136,256]{1,0:T(8,128)S(1)}, f32[136,256]{1,0:T(8,128)S(1)}, u32[]{:S(2)}, u32[]{:S(2)}) collective-permute-start(f32[136,256]{1,0:T(8,128)S(1)} %get-tuple-element.28), channel_id=1, source_target_pairs={{0,1},{1,0},{2,3},{3,2},{4,5},{5,4},{6,7},{7,6},{8,9},{9,8},{10,11... | collective-permute-start | bytes 417800 | tf_op jit(solution)/shard_map/ppermute | solution.py:27
  193.8 20.9 %collective-permute-start.29 = (f32[136,256]{1,0:T(8,128)S(1)}, f32[136,256]{1,0:T(8,128)S(1)}, u32[]{:S(2)}, u32[]{:S(2)}) collective-permute-start(f32[136,256]{1,0:T(8,128)S(1)} %get-tuple-element.26), channel_id=1, source_target_pairs={{0,1},{1,0},{2,3},{3,2},{4,5},{5,4},{6,7},{7,6},{8,9},{9,8},{10,11... | collective-permute-start | bytes 417800 | tf_op jit(solution)/shard_map/ppermute | solution.py:27
  195.7 18.9 %collective-permute-start.41 = (bf16[136,256]{1,0:T(8,128)(2,1)S(1)}, bf16[136,256]{1,0:T(8,128)(2,1)S(1)}, u32[]{:S(2)}, u32[]{:S(2)}) collective-permute-start(bf16[136,256]{1,0:T(8,128)(2,1)S(1)} %fold.3), channel_id=1, source_target_pairs={{0,256},{1,257},{2,258},{3,259},{4,260},{5,261},{6,262},{7,263},{8... | collective-permute-start | bytes 208904 | tf_op jit(solution)/shard_map/ppermute | solution.py:27
  (7 other events, 106.0 us)
